TPU v7x, 32 devices: a whole 2x2x4 slice. The times are simulated.
32 devices in a mesh: seq: 4 (over y, core), ctx: 8 (over z, x).
Axes of the slice: x: 2, y: 2, z: 4, core: 2. Of those that a mesh axis runs over, the one named last changes fastest.
Arguments:
- layer_input: bfloat16 [4, 1024, 1024], P('seq', 'ctx')
- document_ids: int32 [4, 1024], P('seq', 'ctx'), may hold values from 0 to 3, never falling along the last dimension, each value on 1 to 512 neighbouring positions
- expert_routes: int32 [4, 1024, 8], P('seq', 'ctx'), may hold values from 0 to 15, all different within a row; in each aligned block of 128 rows (0 to 127, 128 to 255, ..., all dimensions but the last counted through in order) at most 96 rows name the same one
- rope_factor: float32 [1], replicated, may hold values from 1 to 4
- attention_gain: float32 [1024], P(('seq', 'ctx')), may hold values from 0.25 to 1.75
- feedforward_gain: float32 [1024], P(('seq', 'ctx')), may hold values from 0.25 to 1.75
- query_weight: float32 [1024, 1024], P(('seq', 'ctx')), may hold values from -0.1875 to 0.1875
- key_weight: float32 [1024, 512], P(('seq', 'ctx')), may hold values from -0.1875 to 0.1875
- value_weight: float32 [1024, 512], P(('seq', 'ctx')), may hold values from -0.1875 to 0.1875
- output_weight: float32 [1024, 1024], P(('seq', 'ctx')), may hold values from -1.5 to 1.5
- router_weight: float32 [1024, 16], P(('seq', 'ctx')), may hold values from -0.375 to 0.375
- gate_up: float32 [1024, 16, 1024], P(('seq', 'ctx')), may hold values from -0.1875 to 0.1875
- down_weight: float32 [512, 16, 1024], P(('seq', 'ctx')), may hold values from -0.25 to 0.25
- cotangent: bfloat16 [4, 1024, 1024], P('seq', 'ctx'), may hold values from -6 to 6
Outputs:
- layer_output: bfloat16 [4, 1024, 1024], P('seq', 'ctx')
- input_gradient: bfloat16 [4, 1024, 1024], P('seq', 'ctx')
- attention_gain_gradient: float32 [1024], P(('seq', 'ctx'))
- feedforward_gain_gradient: float32 [1024], P(('seq', 'ctx'))
- query_gradient: float32 [1024, 1024], P(('seq', 'ctx'))
- key_gradient: float32 [1024, 512], P(('seq', 'ctx'))
- value_gradient: float32 [1024, 512], P(('seq', 'ctx'))
- output_gradient: float32 [1024, 1024], P(('seq', 'ctx'))
- router_gradient: float32 [1024, 16], P(('seq', 'ctx'))
- gate_up_gradient: float32 [1024, 16, 1024], P(('seq', 'ctx'))
- down_gradient: float32 [512, 16, 1024], P(('seq', 'ctx'))
Inputs may be any that keep to these rules, and one draw needn't show every extreme that they name: `document_ids`: document ids never fall along a sequence; each of the 4 documents holds 1 to 512 tokens, and one holds exactly 512. `expert_routes`: each token names 8 different experts. Among the 128 tokens of one device (aligned blocks of a sequence) no expert is named by more than 96 tokens, and in some block some expert is named by exactly 96.
All inputs are finite; a program needn't handle non-finite values.
Results may differ from a plain program's by a relative error of at most 0.025.
Values may be sent and summed in bfloat16 or wider, within the bound.
A program may use at most 320 MiB of HBM per device.

v0:
```python
import jax
import jax.numpy as jnp
from jax import lax
from jax.sharding import PartitionSpec as P

HEADS = 16
KV_HEADS = 8
HEAD_DIM = 64
FF = 512
CAP = 96


NORM_EPS = 1e-06
ROPE_BASE = 10000.0
NEG_BIG = -1e30


def rms_scale(values):
    return lax.rsqrt(jnp.mean(values * values, axis=-1, keepdims=True) + NORM_EPS)


def softmax_last(scores):
    row_peak = jnp.max(scores, axis=-1, keepdims=True)
    expo = jnp.exp(scores - row_peak)
    return expo / jnp.sum(expo, axis=-1, keepdims=True)


def rotate_pairs(values, cosine, sine):
    half_dim = values.shape[-1] // 2
    first_half = values[..., :half_dim]
    second_half = values[..., half_dim:]
    return jnp.concatenate(
        [first_half * cosine - second_half * sine, second_half * cosine + first_half * sine],
        axis=-1,
    )


def unrotate_pairs(values, cosine, sine):
    half_dim = values.shape[-1] // 2
    first_half = values[..., :half_dim]
    second_half = values[..., half_dim:]
    return jnp.concatenate(
        [first_half * cosine + second_half * sine, second_half * cosine - first_half * sine],
        axis=-1,
    )


def rope_tables(places, factor):
    freqs = 1.0 / ROPE_BASE ** (jnp.arange(0, HEAD_DIM, 2).astype(jnp.float32) / HEAD_DIM)
    angles = (places.astype(jnp.float32) / factor)[:, None] * freqs[None, :]
    return (jnp.cos(angles)[:, None, :], jnp.sin(angles)[:, None, :])


def keep_state(current_state):
    return current_state


def on_device(
    layer_input,
    document_ids,
    expert_routes,
    rope_factor,
    attention_gain,
    feedforward_gain,
    query_weight,
    key_weight,
    value_weight,
    output_weight,
    router_weight,
    gate_up,
    down_weight,
    cotangent,
):
    tokens_here = layer_input.shape[1]
    model_width = layer_input.shape[2]
    group_size = HEADS // KV_HEADS
    score_scale = HEAD_DIM ** (-0.5)
    experts = router_weight.shape[1]
    top_count = expert_routes.shape[2]
    length = tokens_here * lax.axis_size("ctx")
    per_expert = lax.axis_size(("seq", "ctx")) // experts
    per_peer = CAP // per_expert
    gain_one, gain_two, query_full, key_full, value_full, out_full, router_full = (
        lax.all_gather(attention_gain.astype(jnp.bfloat16), ("seq", "ctx"), axis=0, tiled=True),
        lax.all_gather(feedforward_gain.astype(jnp.bfloat16), ("seq", "ctx"), axis=0, tiled=True),
        lax.all_gather(query_weight.astype(jnp.bfloat16), ("seq", "ctx"), axis=0, tiled=True),
        lax.all_gather(key_weight.astype(jnp.bfloat16), ("seq", "ctx"), axis=0, tiled=True),
        lax.all_gather(value_weight.astype(jnp.bfloat16), ("seq", "ctx"), axis=0, tiled=True),
        lax.all_gather(output_weight.astype(jnp.bfloat16), ("seq", "ctx"), axis=0, tiled=True),
        lax.all_gather(router_weight.astype(jnp.bfloat16), ("seq", "ctx"), axis=0, tiled=True),
    )
    gate_up_low = gate_up.astype(jnp.bfloat16)
    down_low = down_weight.astype(jnp.bfloat16)
    inputs = layer_input[0].astype(jnp.float32)
    scale_one = rms_scale(inputs)
    normed_one = inputs * scale_one
    attend_input = (normed_one * gain_one.astype(jnp.float32)).astype(jnp.bfloat16)
    query_pre = jnp.dot(attend_input, query_full, preferred_element_type=jnp.float32).reshape(
        tokens_here, HEADS, HEAD_DIM
    )
    key_pre = jnp.dot(attend_input, key_full, preferred_element_type=jnp.float32).reshape(
        tokens_here, KV_HEADS, HEAD_DIM
    )
    value_rows = jnp.dot(attend_input, value_full, preferred_element_type=jnp.float32).astype(
        jnp.bfloat16
    )
    own_index = lax.axis_index("ctx")
    query_places = own_index * tokens_here + jnp.arange(tokens_here, dtype=jnp.int32)
    cosine, sine = rope_tables(query_places, rope_factor[0])
    query_rot = rotate_pairs(query_pre, cosine, sine).astype(jnp.bfloat16)
    key_rot = (
        rotate_pairs(key_pre, cosine, sine)
        .astype(jnp.bfloat16)
        .reshape(tokens_here, KV_HEADS * HEAD_DIM)
    )
    queries = query_rot.reshape(tokens_here, KV_HEADS, group_size, HEAD_DIM).transpose(1, 2, 0, 3)
    doc_here = document_ids[0].astype(jnp.bfloat16)
    last_place = query_places[-1]

    def scores_for(keys_block, docs_block, first_key):
        raw_scores = (
            jnp.einsum(
                "kgqd,nkd->kgqn",
                queries,
                keys_block.reshape(-1, KV_HEADS, HEAD_DIM),
                preferred_element_type=jnp.float32,
            )
            * score_scale
        )
        key_places = first_key + jnp.arange(keys_block.shape[0], dtype=jnp.int32)
        allowed = (key_places[None, :] <= query_places[:, None]) & (
            docs_block[None, :] == doc_here[:, None]
        )
        return (raw_scores, allowed)

    start_state = (
        jnp.full((KV_HEADS, group_size, tokens_here), NEG_BIG, jnp.float32),
        jnp.zeros((KV_HEADS, group_size, tokens_here), jnp.float32),
        jnp.zeros((KV_HEADS, group_size, tokens_here, HEAD_DIM), jnp.float32),
    )
    keys_part = lax.all_gather(key_rot, "ctx", axis=0, tiled=True)
    values_part = lax.all_gather(value_rows, "ctx", axis=0, tiled=True)
    docs_part = lax.all_gather(doc_here, "ctx", axis=0, tiled=True)
    piece_rows = keys_part.shape[0]
    block_rows = 512

    def forward_one_block(block_step, current):
        offset = block_step * block_rows

        def forward_compute(current_state):
            row_peak, row_total, weighted_sum = current_state
            keys_block = lax.dynamic_slice_in_dim(keys_part, offset, block_rows, 0)
            values_block = lax.dynamic_slice_in_dim(values_part, offset, block_rows, 0).reshape(
                block_rows, KV_HEADS, HEAD_DIM
            )
            docs_block = lax.dynamic_slice_in_dim(docs_part, offset, block_rows, 0)
            raw_scores, allowed = scores_for(keys_block, docs_block, offset)
            masked = jnp.where(allowed, raw_scores, NEG_BIG)
            new_peak = jnp.maximum(row_peak, jnp.max(masked, axis=-1))
            expo = jnp.where(allowed, jnp.exp(masked - new_peak[..., None]), 0.0)
            shrink = jnp.exp(row_peak - new_peak)
            row_total = row_total * shrink + jnp.sum(expo, axis=-1)
            weighted_sum = weighted_sum * shrink[..., None] + jnp.einsum(
                "kgqn,nkd->kgqd",
                expo.astype(jnp.bfloat16),
                values_block,
                preferred_element_type=jnp.float32,
            )
            return (new_peak, row_total, weighted_sum)

        return lax.cond(offset <= last_place, forward_compute, keep_state, current)

    row_peak, row_total, weighted_sum = lax.fori_loop(
        0, piece_rows // block_rows, forward_one_block, start_state
    )
    attended = weighted_sum / row_total[..., None]
    log_total = row_peak + jnp.log(row_total)
    mixed_low = (
        attended.transpose(2, 0, 1, 3).reshape(tokens_here, HEADS * HEAD_DIM).astype(jnp.bfloat16)
    )
    middle = inputs + jnp.dot(mixed_low, out_full, preferred_element_type=jnp.float32)
    scale_two = rms_scale(middle)
    normed_two = middle * scale_two
    expert_input = (normed_two * gain_two.astype(jnp.float32)).astype(jnp.bfloat16)
    logits = jnp.dot(expert_input, router_full, preferred_element_type=jnp.float32)
    routes_here = expert_routes[0]
    chosen = (
        routes_here[:, :, None] == jnp.arange(experts, dtype=jnp.int32)[None, None, :]
    ).astype(jnp.float32)
    gate_probs = softmax_last(jnp.sum(chosen * logits[:, None, :], axis=-1))
    pair_expert = routes_here.reshape(-1)
    pair_count = pair_expert.shape[0]
    pair_onehot = (pair_expert[:, None] == jnp.arange(experts, dtype=jnp.int32)[None, :]).astype(
        jnp.int32
    )
    slot_rank = jnp.sum((jnp.cumsum(pair_onehot, axis=0) - pair_onehot) * pair_onehot, axis=1)
    pair_slot = pair_expert * CAP + slot_rank % per_expert * per_peer + slot_rank // per_expert
    slot_pair = (
        jnp.full((experts * CAP,), pair_count, jnp.int32)
        .at[pair_slot]
        .set(jnp.arange(pair_count, dtype=jnp.int32))
    )
    slot_token = slot_pair // top_count
    padded_input = jnp.concatenate(
        [expert_input, jnp.zeros((1, model_width), jnp.bfloat16)], axis=0
    )
    slot_rows = padded_input[slot_token].reshape(experts, CAP, model_width)
    columns = slot_rows
    gate_and_up = jnp.einsum(
        "ecr,ref->ecf",
        columns,
        lax.all_gather(gate_up_low, ("seq", "ctx"), axis=0, tiled=True),
        preferred_element_type=jnp.float32,
    )
    gate_part = gate_and_up[..., :FF]
    up_part = gate_and_up[..., FF:]
    gate_sigmoid = 1.0 / (1.0 + jnp.exp(-gate_part))
    activated = gate_part / (1.0 + jnp.exp(-gate_part))
    hidden = (activated * up_part).astype(jnp.bfloat16)
    columns = hidden
    produced = jnp.einsum(
        "ecr,red->ecd",
        columns,
        lax.all_gather(down_low, ("seq", "ctx"), axis=0, tiled=True),
        preferred_element_type=jnp.float32,
    )
    produced = produced.reshape(experts * CAP, model_width)
    pair_out = produced[pair_slot].reshape(tokens_here, top_count, model_width)
    expert_mix = jnp.sum(gate_probs[..., None] * pair_out, axis=1)
    layer_output = (middle + expert_mix).astype(jnp.bfloat16)[None]
    upstream = cotangent[0].astype(jnp.float32)
    gate_weight_grad = jnp.sum(upstream[:, None, :] * pair_out, axis=-1)
    select_grad = gate_probs * (
        gate_weight_grad - jnp.sum(gate_probs * gate_weight_grad, axis=-1, keepdims=True)
    )
    logit_grad = jnp.sum(select_grad[..., None] * chosen, axis=1).astype(jnp.bfloat16)
    pair_grad = (
        (gate_probs[..., None] * upstream[:, None, :])
        .reshape(pair_count, model_width)
        .astype(jnp.bfloat16)
    )
    padded_grad = jnp.concatenate([pair_grad, jnp.zeros((1, model_width), jnp.bfloat16)], axis=0)
    slot_grad = padded_grad[slot_pair].reshape(experts, CAP, model_width)
    hidden_grad = jnp.einsum(
        "ecd,red->ecr",
        slot_grad,
        lax.all_gather(down_low, ("seq", "ctx"), axis=0, tiled=True),
        preferred_element_type=jnp.float32,
    )
    gate_grad = hidden_grad * up_part * gate_sigmoid * (1.0 + gate_part * (1.0 - gate_sigmoid))
    up_grad = hidden_grad * activated
    both_grad = jnp.concatenate([gate_grad, up_grad], axis=-1).astype(jnp.bfloat16)
    columns = hidden
    down_gradient = lax.psum_scatter(
        jnp.einsum("ecr,ecd->red", columns, slot_grad, preferred_element_type=jnp.float32),
        ("seq", "ctx"),
        scatter_dimension=0,
        tiled=True,
    )
    columns = slot_rows
    gate_up_gradient = lax.psum_scatter(
        jnp.einsum("ecr,ecf->ref", columns, both_grad, preferred_element_type=jnp.float32),
        ("seq", "ctx"),
        scatter_dimension=0,
        tiled=True,
    )
    slot_input_grad = jnp.einsum(
        "ecf,ref->ecr",
        both_grad,
        lax.all_gather(gate_up_low, ("seq", "ctx"), axis=0, tiled=True),
        preferred_element_type=jnp.float32,
    )
    slot_input_grad = slot_input_grad.reshape(experts * CAP, model_width)
    pair_input_grad = slot_input_grad[pair_slot].reshape(tokens_here, top_count, model_width)
    input_two_grad = jnp.sum(pair_input_grad, axis=1) + jnp.einsum(
        "te,de->td", logit_grad, router_full, preferred_element_type=jnp.float32
    )
    router_part = jnp.einsum(
        "td,te->de", expert_input, logit_grad, preferred_element_type=jnp.float32
    )
    normed_two_grad = input_two_grad * gain_two.astype(jnp.float32)
    gain_two_part = jnp.sum(input_two_grad * normed_two, axis=0)
    middle_grad = upstream + scale_two * (
        normed_two_grad
        - normed_two * jnp.mean(normed_two_grad * normed_two, axis=-1, keepdims=True)
    )
    projection_grad = middle_grad.astype(jnp.bfloat16)
    out_part = jnp.einsum(
        "tj,td->jd", mixed_low, projection_grad, preferred_element_type=jnp.float32
    )
    mixed_grad = jnp.einsum(
        "td,jd->tj", projection_grad, out_full, preferred_element_type=jnp.float32
    ).astype(jnp.bfloat16)
    mixed_grad_heads = mixed_grad.reshape(tokens_here, KV_HEADS, group_size, HEAD_DIM).transpose(
        1, 2, 0, 3
    )
    row_delta = jnp.sum(mixed_grad_heads.astype(jnp.float32) * attended, axis=-1)
    back_state = (
        jnp.zeros((KV_HEADS, group_size, tokens_here, HEAD_DIM), jnp.float32),
        jnp.zeros((length, KV_HEADS * HEAD_DIM), jnp.float32),
        jnp.zeros((length, KV_HEADS * HEAD_DIM), jnp.float32),
    )
    backward_keys_part = lax.all_gather(key_rot, "ctx", axis=0, tiled=True)
    backward_values_part = lax.all_gather(value_rows, "ctx", axis=0, tiled=True)
    backward_docs_part = lax.all_gather(doc_here, "ctx", axis=0, tiled=True)
    piece_rows = backward_keys_part.shape[0]
    backward_block_rows = 512

    def backward_one_block(block_step, current):
        offset = block_step * backward_block_rows

        def backward_compute(current_state):
            query_grad, key_grads, value_grads = current_state
            keys_block = lax.dynamic_slice_in_dim(
                backward_keys_part, offset, backward_block_rows, 0
            )
            values_block = lax.dynamic_slice_in_dim(
                backward_values_part, offset, backward_block_rows, 0
            ).reshape(backward_block_rows, KV_HEADS, HEAD_DIM)
            docs_block = lax.dynamic_slice_in_dim(
                backward_docs_part, offset, backward_block_rows, 0
            )
            raw_scores, allowed = scores_for(keys_block, docs_block, offset)
            attention_probs = jnp.where(allowed, jnp.exp(raw_scores - log_total[..., None]), 0.0)
            probs_low = attention_probs.astype(jnp.bfloat16)
            value_block_grad = jnp.einsum(
                "kgqn,kgqd->nkd", probs_low, mixed_grad_heads, preferred_element_type=jnp.float32
            )
            prob_grad = jnp.einsum(
                "kgqd,nkd->kgqn", mixed_grad_heads, values_block, preferred_element_type=jnp.float32
            )
            score_grad = (attention_probs * (prob_grad - row_delta[..., None])).astype(jnp.bfloat16)
            query_grad = (
                query_grad
                + jnp.einsum(
                    "kgqn,nkd->kgqd",
                    score_grad,
                    keys_block.reshape(backward_block_rows, KV_HEADS, HEAD_DIM),
                    preferred_element_type=jnp.float32,
                )
                * score_scale
            )
            key_block_grad = (
                jnp.einsum(
                    "kgqn,kgqd->nkd", score_grad, queries, preferred_element_type=jnp.float32
                )
                * score_scale
            )
            key_grads = lax.dynamic_update_slice_in_dim(
                key_grads,
                lax.dynamic_slice_in_dim(key_grads, offset, backward_block_rows, 0)
                + key_block_grad.reshape(backward_block_rows, -1),
                offset,
                0,
            )
            value_grads = lax.dynamic_update_slice_in_dim(
                value_grads,
                lax.dynamic_slice_in_dim(value_grads, offset, backward_block_rows, 0)
                + value_block_grad.reshape(backward_block_rows, -1),
                offset,
                0,
            )
            return (query_grad, key_grads, value_grads)

        return lax.cond(offset <= last_place, backward_compute, keep_state, current)

    query_grad, key_grads, value_grads = lax.fori_loop(
        0, piece_rows // backward_block_rows, backward_one_block, back_state
    )
    key_grad_here, value_grad_here = (
        lax.psum_scatter(
            key_grads.astype(jnp.bfloat16), "ctx", scatter_dimension=0, tiled=True
        ).astype(jnp.float32),
        lax.psum_scatter(
            value_grads.astype(jnp.bfloat16), "ctx", scatter_dimension=0, tiled=True
        ).astype(jnp.float32),
    )
    query_rows_grad = query_grad.transpose(2, 0, 1, 3).reshape(tokens_here, HEADS, HEAD_DIM)
    query_pre_grad = (
        unrotate_pairs(query_rows_grad, cosine, sine)
        .reshape(tokens_here, HEADS * HEAD_DIM)
        .astype(jnp.bfloat16)
    )
    key_pre_grad = (
        unrotate_pairs(key_grad_here.reshape(tokens_here, KV_HEADS, HEAD_DIM), cosine, sine)
        .reshape(tokens_here, KV_HEADS * HEAD_DIM)
        .astype(jnp.bfloat16)
    )
    value_pre_grad = value_grad_here.astype(jnp.bfloat16)
    query_part = jnp.einsum(
        "td,tj->dj", attend_input, query_pre_grad, preferred_element_type=jnp.float32
    )
    key_part = jnp.einsum(
        "td,tj->dj", attend_input, key_pre_grad, preferred_element_type=jnp.float32
    )
    value_part = jnp.einsum(
        "td,tj->dj", attend_input, value_pre_grad, preferred_element_type=jnp.float32
    )
    attend_grad = (
        jnp.einsum("tj,dj->td", query_pre_grad, query_full, preferred_element_type=jnp.float32)
        + jnp.einsum("tj,dj->td", key_pre_grad, key_full, preferred_element_type=jnp.float32)
        + jnp.einsum("tj,dj->td", value_pre_grad, value_full, preferred_element_type=jnp.float32)
    )
    normed_one_grad = attend_grad * gain_one.astype(jnp.float32)
    gain_one_part = jnp.sum(attend_grad * normed_one, axis=0)
    input_gradient = (
        middle_grad
        + scale_one
        * (
            normed_one_grad
            - normed_one * jnp.mean(normed_one_grad * normed_one, axis=-1, keepdims=True)
        )
    ).astype(jnp.bfloat16)[None]
    (
        gain_one_grad,
        gain_two_grad,
        query_gradient,
        key_gradient,
        value_gradient,
        output_gradient,
        router_gradient,
    ) = (
        lax.psum_scatter(gain_one_part, ("seq", "ctx"), scatter_dimension=0, tiled=True),
        lax.psum_scatter(gain_two_part, ("seq", "ctx"), scatter_dimension=0, tiled=True),
        lax.psum_scatter(query_part, ("seq", "ctx"), scatter_dimension=0, tiled=True),
        lax.psum_scatter(key_part, ("seq", "ctx"), scatter_dimension=0, tiled=True),
        lax.psum_scatter(value_part, ("seq", "ctx"), scatter_dimension=0, tiled=True),
        lax.psum_scatter(out_part, ("seq", "ctx"), scatter_dimension=0, tiled=True),
        lax.psum_scatter(router_part, ("seq", "ctx"), scatter_dimension=0, tiled=True),
    )
    return (
        layer_output,
        input_gradient,
        gain_one_grad,
        gain_two_grad,
        query_gradient,
        key_gradient,
        value_gradient,
        output_gradient,
        router_gradient,
        gate_up_gradient,
        down_gradient,
    )


def solution(mesh):
    return jax.shard_map(
        on_device,
        mesh=mesh,
        in_specs=(
            P("seq", "ctx", None),
            P("seq", "ctx"),
            P("seq", "ctx", None),
            P(),
            P(("seq", "ctx")),
            P(("seq", "ctx")),
            P(("seq", "ctx"), None),
            P(("seq", "ctx"), None),
            P(("seq", "ctx"), None),
            P(("seq", "ctx"), None),
            P(("seq", "ctx"), None),
            P(("seq", "ctx"), None, None),
            P(("seq", "ctx"), None, None),
            P("seq", "ctx", None),
        ),
        out_specs=(
            P("seq", "ctx", None),
            P("seq", "ctx", None),
            P(("seq", "ctx")),
            P(("seq", "ctx")),
            P(("seq", "ctx"), None),
            P(("seq", "ctx"), None),
            P(("seq", "ctx"), None),
            P(("seq", "ctx"), None),
            P(("seq", "ctx"), None),
            P(("seq", "ctx"), None, None),
            P(("seq", "ctx"), None, None),
        ),
        check_vma=False,
    )
```

profile of v0, /device:TPU:0, one launch (start us, length us, event | category | flops | bytes accessed | tf_op | source)
XLA Modules:
  0.0 3691.1 jit_solution(9166017817708158678)
XLA Ops:
  7.2 1.5 convert_element_type.216
  8.8 1.5 convert_element_type.210
  12.1 42.1 %all-reduce.7 = (bf16[1024]{0:T(1024)(128)(2,1)S(1)}, bf16[1024]{0:T(1024)(128)(2,1)S(1)}) all-reduce(bf16[1024]{0:T(1024)(128)(2,1)S(1)} %dynamic-update-slice, bf16[1024]{0:T(1024)(128)(2,1)S(1)} %dynamic-update-slice.1), channel_id=1, replica_groups=mesh['seq'=4,'ctx'=8] {'seq','ctx'}, use_global_device_ids=true, to_apply=%add.2 | all-reduce | flops 2048 | bytes 8192
  55.3 12.9 all-gather.17.cloned.1.call-done
  68.1 2.3 convolution_convert_fusion.1
  70.5 1.5 convert_element_type.214
  73.0 51.5 %all-gather.11.cloned.1.call-done = bf16[1024,512]{1,0:T(8,128)(2,1)} async-done(((bf16[32,512]{1,0:T(8,128)(2,1)}), bf16[1024,512]{1,0:T(8,128)(2,1)}) %all-gather.11.cloned.1.call-update) | async-done | bytes 1048592 | tf_op jit(solution)/shard_map/all_gather | solution.py:87
  124.5 1.5 copy.109
  127.3 1.5 convert_element_type.221
  129.0 2.1 copy.148
  131.2 2.6 copy.149
  135.0 4.5 reduce-window.6
  139.8 67.4 %all-gather.1 = bf16[32,32,16]{1,2,0:T(8,128)(2,1)S(1)} all-gather(bf16[1,32,16]{1,2,0:T(8,128)(2,1)S(1)} %convert_bitcast_fusion.1), channel_id=1, replica_groups=mesh['seq'=4,'ctx'=8] {'seq','ctx'}, dimensions={0}, use_global_device_ids=true | all-gather | bytes 33792 | tf_op jit(solution)/shard_map/all_gather | solution.py:90
  207.4 16.3 all-gather
  223.9 4.3 scatter_custom_fusion
  229.1 1.9 copy.111
  231.1 2.9 copy.110
  234.9 31.0 all-gather.13.cloned.1.call-done
  266.0 5.9 while.36
  266.6 4.6 conditional.6
  272.0 52.9 %all-gather.21.cloned.1.call-done = bf16[1024,1024]{1,0:T(8,128)(2,1)} async-done(((bf16[32,1024]{1,0:T(8,128)(2,1)}), bf16[1024,1024]{1,0:T(8,128)(2,1)}) %all-gather.21.cloned.1.call-update) | async-done | bytes 2097168 | tf_op jit(solution)/shard_map/all_gather | solution.py:89
  324.8 2.1 multiply_reduce_fusion.3
  329.4 5.8 gather_fusion.2
  335.2 5.9 gather_fusion
  341.0 180.0 %all-gather.23.cloned.1.call-done = bf16[1024,16,1024]{2,0,1:T(8,128)(2,1)} async-done(((bf16[32,16,1024]{2,0,1:T(8,128)(2,1)}), bf16[1024,16,1024]{2,0,1:T(8,128)(2,1)}) %all-gather.23.cloned.1.call-update) | async-done | bytes 33554448 | tf_op jit(solution)/shard_map/all_gather | solution.py:212
  521.0 19.9 fusion.90
  540.9 96.5 %all-gather.25.cloned.1.call-done = bf16[512,16,1024]{2,0,1:T(8,128)(2,1)} async-done(((bf16[16,16,1024]{2,0,1:T(8,128)(2,1)}), bf16[512,16,1024]{2,0,1:T(8,128)(2,1)}) %all-gather.25.cloned.1.call-update) | async-done | bytes 16777232 | tf_op jit(solution)/shard_map/all_gather | solution.py:224
  637.4 12.8 multiply_convert_fusion.1
  650.2 18.8 fusion.32
  669.0 9.2 gather_fusion.3
  678.2 4.0 bitcast_reduce_fusion
  682.2 11.2 fusion.91
  693.4 9.5 gather_fusion.1
  702.9 4.6 fusion.30
  707.6 2.3 multiply_reduce_fusion
  709.9 2.1 multiply_add_fusion.1
  716.1 1.6 broadcast.387
  717.7 10.7 while.37
  718.4 9.4 conditional.7
  722.5 1.5 fusion.16
  733.3 68.8 %reduce-scatter.30.cloned.1.call-done = bf16[128,512]{1,0:T(8,128)(2,1)} async-done(((bf16[1024,512]{1,0:T(8,128)(2,1)}), bf16[128,512]{1,0:T(8,128)(2,1)}) %reduce-scatter.30.cloned.1.call-update) | async-done | bytes 131088
  802.1 2.7 fusion.63
  805.0 64.2 %reduce-scatter.28.cloned.1.call-done = bf16[128,512]{1,0:T(8,128)(2,1)} async-done(((bf16[1024,512]{1,0:T(8,128)(2,1)}), bf16[128,512]{1,0:T(8,128)(2,1)}) %reduce-scatter.28.cloned.1.call-update) | async-done | bytes 131088
  870.3 1.9 fusion.55
  872.3 2.8 fusion.60
  876.9 2.8 fusion.57
  879.8 1.8 copy-done.6
  881.6 14.8 convolution_bitcast_fusion.2
  896.4 33.2 copy.127
  929.7 1.8 copy-done.4
  931.5 25.1 convolution_bitcast_fusion.1
  956.6 65.7 %copy.126 = f32[1024,16,1024]{2,1,0:T(8,128)} copy(f32[1024,16,1024]{0,2,1:T(8,128)} %convolution_bitcast_fusion.1) | data formatting | bytes 134217728 | tf_op jit(solution)/shard_map/ecr,ecf->ref/transpose | solution.py:262
  1022.3 1.6 copy-done.11
  1023.9 1.6 fusion.92
  1025.5 1.4 copy.143
  1026.9 1.8 convolution_add_fusion.1
  1028.8 1.9 fusion.45
  1030.7 40.1 %all-reduce.6 = (f32[1024]{0:T(1024)S(1)}, f32[1024]{0:T(1024)S(1)}) all-reduce(f32[1024]{0:T(1024)S(1)} %get-tuple-element.752, f32[1024]{0:T(1024)S(1)} %copy-done.37), channel_id=5, replica_groups=mesh['seq'=4,'ctx'=8] {'seq','ctx'}, use_global_device_ids=true, to_apply=%region_30.31.clone | all-reduce | flops 2048 | bytes 16384
  1072.9 71.5 %reduce-scatter.20.cloned.1.call-done = f32[32,512]{1,0:T(8,128)} async-done(((f32[1024,512]{1,0:T(8,128)}), f32[32,512]{1,0:T(8,128)}) %reduce-scatter.20.cloned.1.call-update) | async-done | bytes 65552 | tf_op jit(solution)/shard_map/reduce_scatter | solution.py:427
  1144.4 139.2 %reduce-scatter.18.cloned.1.call-done = f32[32,512]{1,0:T(8,128)} async-done(((f32[1024,512]{1,0:T(8,128)}), f32[32,512]{1,0:T(8,128)}) %reduce-scatter.18.cloned.1.call-update) | async-done | bytes 65552 | tf_op jit(solution)/shard_map/reduce_scatter | solution.py:426
  1283.6 144.2 %reduce-scatter.22.cloned.1.call-done = f32[32,1024]{1,0:T(8,128)} async-done(((f32[1024,1024]{1,0:T(8,128)}), f32[32,1024]{1,0:T(8,128)}) %reduce-scatter.22.cloned.1.call-update) | async-done | bytes 131088 | tf_op jit(solution)/shard_map/reduce_scatter | solution.py:428
  1427.8 145.4 %reduce-scatter.16.cloned.1.call-done = f32[32,1024]{1,0:T(8,128)} async-done(((f32[1024,1024]{1,0:T(8,128)}), f32[32,1024]{1,0:T(8,128)}) %reduce-scatter.16.cloned.1.call-update) | async-done | bytes 131088 | tf_op jit(solution)/shard_map/reduce_scatter | solution.py:425
  1573.3 705.7 %reduce-scatter.26.cloned.1.call-done = f32[16,16,1024]{2,1,0:T(8,128)} async-done(((f32[512,16,1024]{2,1,0:T(8,128)}), f32[16,16,1024]{2,1,0:T(8,128)}) %reduce-scatter.26.cloned.1.call-update) | async-done | bytes 1048592 | tf_op jit(solution)/shard_map/reduce_scatter | solution.py:254
  2278.9 1405.3 %reduce-scatter.24.cloned.1.call-done = f32[32,16,1024]{2,1,0:T(8,128)} async-done(((f32[1024,16,1024]{2,1,0:T(8,128)}), f32[32,16,1024]{2,1,0:T(8,128)}) %reduce-scatter.24.cloned.1.call-update) | async-done | bytes 2097168 | tf_op jit(solution)/shard_map/reduce_scatter | solution.py:261
  (230 shorter events, 37.5 us)
Async XLA Ops:
  7.2 118.9 %copy-start.5 = (bf16[1,128,1024]{2,1,0:T(8,128)(2,1)S(1)}, bf16[1,128,1024]{2,1,0:T(8,128)(2,1)}, u32[]{:S(2)}) copy-start(bf16[1,128,1024]{2,1,0:T(8,128)(2,1)} %param.22) | copy-start | bytes 786436
  7.2 61.0 %all-gather.17.cloned.1.call-start = ((), (), s32[]{:S(2)}) async-start(), calls=%async_computation.12 | async-start | bytes 1081344 | tf_op jit(solution)/shard_map/all_gather | solution.py:88
  8.8 115.8 %all-gather.11.cloned.1.call-start = ((), (), s32[]{:S(2)}) async-start(), calls=%async_computation.9 | async-start | bytes 1081344 | tf_op jit(solution)/shard_map/all_gather | solution.py:87
  10.3 218.9 %all-gather.19.cloned.1.call-start = ((), (), s32[]{:S(2)}) async-start(), calls=%async_computation.13 | async-start | bytes 1179648 | tf_op jit(solution)/shard_map/all_gather | solution.py:142
  54.1 179.9 %copy-start.32 = (f32[1024]{0:T(1024)}, f32[1024]{0:T(1024)S(1)}, u32[]{:S(2)}) copy-start(f32[1024]{0:T(1024)S(1)} %convert_element_type.207) | copy-start | bytes 12292
  55.3 178.7 %copy-start.35 = (f32[128]{0:T(128)}, f32[128]{0:T(128)S(1)}, u32[]{:S(2)}) copy-start(f32[128]{0:T(128)S(1)} %add_rsqrt_fusion.1) | copy-start | bytes 1540
  55.3 73.7 %copy-start.25 = (f32[32,16,1024]{2,1,0:T(8,128)S(1)}, f32[32,16,1024]{2,1,0:T(8,128)}, u32[]{:S(2)}) copy-start(f32[32,16,1024]{2,1,0:T(8,128)} %param.33) | copy-start | bytes 6291460
  70.5 160.6 %all-gather.15.cloned.1.call-start = ((), (), s32[]{:S(2)}) async-start(), calls=%async_computation.11 | async-start | bytes 2162688 | tf_op jit(solution)/shard_map/all_gather | solution.py:86
  72.1 193.8 %all-gather.13.cloned.1.call-start = ((), (), s32[]{:S(2)}) async-start(), calls=%async_computation.10 | async-start | bytes 1179648 | tf_op jit(solution)/shard_map/all_gather | solution.py:141
  73.0 161.8 %copy-start.28 = (f32[128,32]{0,1:T(8,128)}, f32[128,32]{0,1:T(8,128)S(1)}, u32[]{:S(2)}) copy-start(f32[128,32]{0,1:T(8,128)S(1)} %get-tuple-element.831) | copy-start | bytes 49156
  73.0 161.8 %copy-start.30 = (f32[128,32]{0,1:T(8,128)}, f32[128,32]{0,1:T(8,128)S(1)}, u32[]{:S(2)}) copy-start(f32[128,32]{0,1:T(8,128)S(1)} %get-tuple-element.832) | copy-start | bytes 49156
  127.3 197.5 %all-gather.21.cloned.1.call-start = ((), (), s32[]{:S(2)}) async-start(), calls=%async_computation.14 | async-start | bytes 2162688 | tf_op jit(solution)/shard_map/all_gather | solution.py:89
  128.9 4.9 copy-start.34
  128.9 10.9 copy-start.38
  128.9 78.5 %copy-start.39 = (s32[1,128]{1,0:T(1,128)S(1)}, s32[1,128]{1,0:T(1,128)}, u32[]{:S(2)}) copy-start(s32[1,128]{1,0:T(1,128)} %param.23) | copy-start | bytes 1540
  129.0 392.1 %all-gather.23.cloned.1.call-start = ((), (), s32[]{:S(2)}) async-start(), calls=%async_computation.15 | async-start | bytes 34603008 | tf_op jit(solution)/shard_map/all_gather | solution.py:212
  131.1 97.2 %copy-start.26 = (bf16[1,128,1024]{2,1,0:T(8,128)(2,1)S(1)}, bf16[1,128,1024]{2,1,0:T(8,128)(2,1)}, u32[]{:S(2)}) copy-start(bf16[1,128,1024]{2,1,0:T(8,128)(2,1)} %param.35) | copy-start | bytes 786436
  131.1 506.3 %all-gather.25.cloned.1.call-start = ((), (), s32[]{:S(2)}) async-start(), calls=%async_computation.16 | async-start | bytes 17301504 | tf_op jit(solution)/shard_map/all_gather | solution.py:224
  133.8 668.3 %reduce-scatter.30.cloned.1.call-start = ((), (), s32[]{:S(2)}) async-start(), calls=%async_computation.24 | async-start | bytes 1179648
  271.9 55.6 %copy-start.3 = (bf16[1024,512]{0,1:T(8,128)(2,1)}, bf16[1024,512]{0,1:T(8,128)(2,1)S(1)}, u32[]{:S(2)}) copy-start(bf16[1024,512]{0,1:T(8,128)(2,1)S(1)} %get-tuple-element.1131) | copy-start | bytes 3145732
  271.9 55.8 %copy-start.17 = (f32[8,2,128,64]{2,3,1,0:T(8,128)}, f32[8,2,128,64]{2,3,1,0:T(8,128)S(1)}, u32[]{:S(2)}) copy-start(f32[8,2,128,64]{2,3,1,0:T(8,128)S(1)} %get-tuple-element.527) | copy-start | bytes 1572868
  272.0 55.0 %copy-start.21 = (bf16[8,2,128,64]{2,3,1,0:T(8,128)(2,1)}, bf16[8,2,128,64]{2,3,1,0:T(8,128)(2,1)S(1)}, u32[]{:S(2)}) copy-start(bf16[8,2,128,64]{2,3,1,0:T(8,128)(2,1)S(1)} %fusion.59) | copy-start | bytes 786436
  327.0 0.8 copy-start.16
  327.1 0.7 copy-start.19
  650.2 32.0 copy-start.10
  693.4 9.5 copy-start.18
  702.9 7.0 copy-start.27
  707.5 5.4 copy-start.12
  712.1 0.8 copy-start.13
  722.5 1.5 copy-start.7
  724.0 1.8 copy-start
  724.5 1.9 copy-start.8
  726.4 1.3 copy-start.1
  728.6 2.0 copy-start.2
  730.0 139.2 %reduce-scatter.28.cloned.1.call-start = ((), (), s32[]{:S(2)}) async-start(), calls=%async_computation.23 | async-start | bytes 1179648
  730.6 71.5 %copy-start.33 = (f32[1024]{0:T(1024)S(1)}, f32[1024]{0:T(1024)}, u32[]{:S(2)}) copy-start(f32[1024]{0:T(1024)} %copy-done.32) | copy-start | bytes 12292
  730.6 71.5 %copy-start.36 = (f32[128]{0:T(128)S(1)}, f32[128]{0:T(128)}, u32[]{:S(2)}) copy-start(f32[128]{0:T(128)} %copy-done.35) | copy-start | bytes 1540
  730.7 1.4 copy-start.20
  732.1 138.1 %copy-start.29 = (f32[128,32]{0,1:T(8,128)S(1)}, f32[128,32]{0,1:T(8,128)}, u32[]{:S(2)}) copy-start(f32[128,32]{0,1:T(8,128)} %copy-done.28) | copy-start | bytes 49156
  732.1 138.1 %copy-start.31 = (f32[128,32]{0,1:T(8,128)S(1)}, f32[128,32]{0,1:T(8,128)}, u32[]{:S(2)}) copy-start(f32[128,32]{0,1:T(8,128)} %copy-done.30) | copy-start | bytes 49156
  732.1 293.4 %reduce-scatter.32.cloned.1.call-start = ((), (), s32[]{:S(2)}) async-start(), calls=%async_computation.25 | async-start | bytes 540672
  733.3 411.1 %reduce-scatter.20.cloned.1.call-start = ((), (), s32[]{:S(2)}) async-start(), calls=%async_computation.19 | async-start | bytes 2162688 | tf_op jit(solution)/shard_map/reduce_scatter | solution.py:427
  804.9 67.4 %copy-start.14 = (f32[128,1024]{1,0:T(8,128)S(1)}, f32[128,1024]{1,0:T(8,128)}, u32[]{:S(2)}) copy-start(f32[128,1024]{1,0:T(8,128)} %copy-done.13) | copy-start | bytes 1572868
  804.9 67.4 %copy-start.22 = (bf16[8,2,128,64]{2,3,1,0:T(8,128)(2,1)S(1)}, bf16[8,2,128,64]{2,3,1,0:T(8,128)(2,1)}, u32[]{:S(2)}) copy-start(bf16[8,2,128,64]{2,3,1,0:T(8,128)(2,1)} %copy-done.21) | copy-start | bytes 786436
  804.9 478.7 %reduce-scatter.18.cloned.1.call-start = ((), (), s32[]{:S(2)}) async-start(), calls=%async_computation.18 | async-start | bytes 2162688 | tf_op jit(solution)/shard_map/reduce_scatter | solution.py:426
  872.2 555.6 %reduce-scatter.22.cloned.1.call-start = ((), (), s32[]{:S(2)}) async-start(), calls=%async_computation.20 | async-start | bytes 4325376 | tf_op jit(solution)/shard_map/reduce_scatter | solution.py:428
  875.0 1.0 copy-start.9
  875.1 698.2 %reduce-scatter.16.cloned.1.call-start = ((), (), s32[]{:S(2)}) async-start(), calls=%async_computation.17 | async-start | bytes 4325376 | tf_op jit(solution)/shard_map/reduce_scatter | solution.py:425
  876.2 0.7 copy-start.23
  879.7 1.9 copy-start.6
  879.7 1399.2 %reduce-scatter.26.cloned.1.call-start = ((), (), s32[]{:S(2)}) async-start(), calls=%async_computation.22 | async-start | bytes 34603008 | tf_op jit(solution)/shard_map/reduce_scatter | solution.py:254
  929.6 1.9 copy-start.4
  929.6 2754.6 %reduce-scatter.24.cloned.1.call-start = ((), (), s32[]{:S(2)}) async-start(), calls=%async_computation.21 | async-start | bytes 69206016 | tf_op jit(solution)/shard_map/reduce_scatter | solution.py:261
  1022.3 1.6 copy-start.11
  1022.3 1.6 copy-start.24
  1023.9 6.8 copy-start.37
  1023.9 48.1 %copy-start.15 = (f32[128,1024]{1,0:T(8,128)S(1)}, f32[128,1024]{1,0:T(8,128)}, u32[]{:S(2)}) copy-start(f32[128,1024]{1,0:T(8,128)} %copy-done.13) | copy-start | bytes 1572868
Sparse Core Ops, SparseCore 0:
  11.6 56.5 all-gather.16
  71.7 52.7 all-gather.10
  127.2 39.6 all-gather.18
  170.3 54.7 all-gather.14
  227.7 38.2 all-gather.12
  269.3 55.4 all-gather.20
  328.5 192.5 all-gather.22
  524.1 113.2 all-gather.24
  730.1 71.9 reduce-scatter.29
  805.9 63.1 reduce-scatter.27
  871.4 134.8 reduce-scatter.31
  1009.0 135.3 reduce-scatter.19
  1147.3 136.3 reduce-scatter.17
  1286.3 141.4 reduce-scatter.21
  1430.5 142.7 reduce-scatter.15
  1576.0 702.9 reduce-scatter.25
  2281.7 1402.5 reduce-scatter.23
where the time goes:
time: 3700 us; the launch traced here: 3690 us
  waiting for transfers between devices  3170 us (86%)
  local copies, waits for them, and re-layouts  170 us (5%)
  blocking collectives  166 us (4%)
  matrix products  135 us (4%)
    reduce_scatter x1, waiting for transfers between devices, on_device(): lax.psum_scatter(jnp.einsum('ecr,ecf->ref', columns, both_grad, preferred...  1410 us
    reduce_scatter x1, waiting for transfers between devices, on_device(): lax.psum_scatter(jnp.einsum('ecr,ecd->red', columns, slot_grad, preferred...  706 us
    all_gather x1, waiting for transfers between devices, on_device(): lax.all_gather(gate_up_low, ('seq', 'ctx'), axis=0, tiled=True)  180 us
    reduce_scatter x1, waiting for transfers between devices, on_device(): lax.psum_scatter(query_part, ('seq', 'ctx'), scatter_dimension=0, tiled=T...  145 us
    reduce_scatter x1, waiting for transfers between devices, on_device(): lax.psum_scatter(out_part, ('seq', 'ctx'), scatter_dimension=0, tiled=True)  144 us
    reduce_scatter x1, waiting for transfers between devices, on_device(): lax.psum_scatter(key_part, ('seq', 'ctx'), scatter_dimension=0, tiled=True)  139 us
    unnamed x20, waiting for transfers between devices  133 us
    all_gather x1, waiting for transfers between devices, on_device(): lax.all_gather(down_low, ('seq', 'ctx'), axis=0, tiled=True)  96.5 us
  transfers between devices with their start and end apart: 17, of which 14 were waited for; matrix products, arithmetic and copies ran while one was open for 6% of the time, Pallas kernels for 0%

commit v1 on v0

v1 whole, which is shorter than its diff:
```python
import functools
import math

import jax
import jax.numpy as jnp
from jax import lax
from jax.experimental import pallas as pl
from jax.experimental.pallas import tpu as pltpu
from jax.sharding import PartitionSpec as P

HEADS = 16
KV_HEADS = 8
HEAD_DIM = 64
GROUP = HEADS // KV_HEADS
HEAD_COLS = (GROUP + 2) * HEAD_DIM

NORM_EPS = 1e-06
ROPE_BASE = 10000.0
NEG_BIG = -1e30
LOW = jnp.bfloat16
WIDE = jnp.float32
MESH = pl.DeviceIdType.MESH


def ring_place(index, size):
    half = index // 2
    return half + (index % 2) * (size - 1 - 2 * half)


def ring_member(place, size):
    place = (place + 2 * size) % size
    far = place // (size // 2)
    return 2 * place + far * (2 * size - 1 - 4 * place)


def core_mate(index):
    return index + 1 - 2 * (index % 2)


def row_mate(index):
    return (index + 2) % 4


def push(src, dst, send, recv, **where):
    return pltpu.make_async_remote_copy(
        src_ref=src, dst_ref=dst, send_sem=send, recv_sem=recv, device_id=where, device_id_type=MESH
    )


def greet(peers):
    barrier = pltpu.get_barrier_semaphore()
    for where in peers:
        pl.semaphore_signal(barrier, inc=1, device_id=where, device_id_type=MESH)
    pl.semaphore_wait(barrier, len(peers))


def ring_peers(size):
    place = ring_place(lax.axis_index("ctx"), size)
    return ring_member(place + 1, size), ring_member(place - 1, size)


class RingGather:
    def __init__(self, size, source, target, send, recv):
        self.size, self.source, self.target, self.send, self.recv = size, source, target, send, recv
        self.me = lax.axis_index("ctx")
        self.place = ring_place(self.me, size)
        self.right, self.left = ring_peers(size)
        self.steps = size // 2

    def _copy(self, way, step, owner_place, use_source):
        owner = ring_member(owner_place, self.size)
        rows = self.source.shape[0]
        part = pl.ds(0, rows)
        if step == self.steps - 1:
            part = pl.ds(0, rows // 2) if way == 0 else pl.ds(rows // 2, rows // 2)
        dst = self.target.at[owner, part]
        src = self.source.at[part] if use_source else dst
        where = self.right if way == 0 else self.left
        return push(src, dst, self.send.at[way, step], self.recv.at[way, step], ctx=where)

    def outgoing(self, way, step):
        place = self.place - step if way == 0 else self.place + step
        return self._copy(way, step, place, step == 0)

    def incoming(self, way, step):
        place = self.place - 1 - step if way == 0 else self.place + 1 + step
        return self._copy(way, step, place, False)

    def start(self, step):
        for way in range(2):
            if step:
                self.incoming(way, step - 1).wait_recv()
            self.outgoing(way, step).start()

    def finish(self):
        for way in range(2):
            self.incoming(way, self.steps - 1).wait_recv()
            for step in range(self.steps):
                self.outgoing(way, step).wait_send()


def gather_kernel(size, count, *refs):
    sources, targets = refs[:count], refs[count : 2 * count]
    send, recv, own = refs[2 * count :]
    me = lax.axis_index("ctx")
    greet([{"ctx": where} for where in ring_peers(size)])
    rings, copies = [], []
    for i in range(count):
        copies.append(pltpu.make_async_copy(sources[i], targets[i].at[me], own.at[i]))
        copies[-1].start()
        rings.append(RingGather(size, sources[i], targets[i], send.at[i], recv.at[i]))
    for step in range(size // 2):
        for ring in rings:
            ring.start(step)
    for ring in rings:
        ring.finish()
    for copy in copies:
        copy.wait()


def gather_ctx(arrays, size, collective):
    count = len(arrays)
    return pl.pallas_call(
        functools.partial(gather_kernel, size, count),
        out_shape=[jax.ShapeDtypeStruct((size,) + a.shape, a.dtype) for a in arrays],
        in_specs=[pl.BlockSpec(memory_space=pl.ANY)] * count,
        out_specs=[pl.BlockSpec(memory_space=pl.ANY)] * count,
        scratch_shapes=[
            pltpu.SemaphoreType.DMA((count, 2, size // 2)),
            pltpu.SemaphoreType.DMA((count, 2, size // 2)),
            pltpu.SemaphoreType.DMA((count,)),
        ],
        compiler_params=pltpu.CompilerParams(collective_id=collective, has_side_effects=True),
        name="gather_ctx_%d" % collective,
    )(*arrays)


class RingReduce:
    def __init__(self, size, own, held, out_buf, send, recv):
        self.size, self.own, self.held, self.out_buf = size, own, held, out_buf
        self.send, self.recv = send, recv
        self.me = lax.axis_index("ctx")
        self.place = ring_place(self.me, size)
        self.right, self.left = ring_peers(size)
        self.steps = size // 2
        self.rows = own.shape[1]

    def _part(self, way, step):
        half = self.rows // 2
        if step:
            return pl.ds(0, self.rows)
        return pl.ds(0, half) if way == 0 else pl.ds(half, half)

    def _owner(self, way, step):
        ahead = self.steps - step
        return ring_member(self.place + ahead if way == 0 else self.place - ahead, self.size)

    def _copy(self, way, step):
        part = self._part(way, step)
        src = self.out_buf.at[way, step - 1] if step else self.own.at[self._owner(way, 0), part]
        where = self.right if way == 0 else self.left
        return push(src, self.held.at[way, step, part], self.send.at[way, step], self.recv.at[way, step], ctx=where)

    def start(self, step):
        for way in range(2):
            if step:
                self._copy(way, step - 1).wait_recv()
                owner = self._owner(way, step)
                if step == 1:
                    half = self.rows // 2
                    near = pl.ds(0, half) if way == 0 else pl.ds(half, half)
                    far = pl.ds(half, half) if way == 0 else pl.ds(0, half)
                    total = self.own[owner, near].astype(WIDE) + self.held[way, 0, near].astype(WIDE)
                    self.out_buf[way, 0, near] = total.astype(LOW)
                    self.out_buf[way, 0, far] = self.own[owner, far]
                else:
                    total = self.own[owner].astype(WIDE) + self.held[way, step - 1].astype(WIDE)
                    self.out_buf[way, step - 1] = total.astype(LOW)
            self._copy(way, step).start()

    def finish(self, target):
        last = self.steps - 1
        for way in range(2):
            self._copy(way, last).wait_recv()
        target[...] = (
            self.own[self.me].astype(WIDE) + self.held[0, last].astype(WIDE) + self.held[1, last].astype(WIDE)
        )
        for way in range(2):
            for step in range(self.steps):
                self._copy(way, step).wait_send()


def reduce_kernel(size, count, extra, *refs):
    n_in = count + extra
    own, target = refs[:count], refs[n_in : n_in + count]
    scratch = refs[2 * n_in :]
    held, out_buf, send, recv = scratch[:count], scratch[count : 2 * count], scratch[2 * count], scratch[2 * count + 1]
    me = lax.axis_index("ctx")
    right, left = ring_peers(size)
    if extra:
        greet([{"ctx": (me + k) % size} for k in range(1, size)])
    else:
        greet([{"ctx": right}, {"ctx": left}])
    direct = []
    if extra:
        source, spread = refs[count], refs[n_in + count]
        send_small, recv_small = scratch[2 * count + 2 :]
        spread[me] = source[me]
        for k in range(1, size):
            there = (me + k) % size
            direct.append(push(source.at[there], spread.at[me], send_small.at[k], recv_small.at[k], ctx=there))
            direct[-1].start()
    rings = [RingReduce(size, own[i], held[i], out_buf[i], send.at[i], recv.at[i]) for i in range(count)]
    for step in range(size // 2):
        for ring in rings:
            ring.start(step)
    for ring, where in zip(rings, target):
        ring.finish(where)
    if extra:
        for k in range(1, size):
            here = (me + size - k) % size
            push(source.at[here], spread.at[here], send_small.at[k], recv_small.at[k], ctx=here).wait_recv()
        for copy in direct:
            copy.wait_send()


def reduce_ctx(arrays, size, collective, small=None):
    count = len(arrays)
    extra = 0 if small is None else 1
    operands = list(arrays) + ([small] if extra else [])
    shapes = [jax.ShapeDtypeStruct(a.shape[1:], WIDE) for a in arrays]
    scratch = [pltpu.VMEM((2, size // 2) + a.shape[1:], LOW) for a in arrays]
    scratch += [pltpu.VMEM((2, size // 2 - 1) + a.shape[1:], LOW) for a in arrays]
    scratch += [pltpu.SemaphoreType.DMA((count, 2, size // 2))] * 2
    if extra:
        shapes.append(jax.ShapeDtypeStruct(small.shape, small.dtype))
        scratch += [pltpu.SemaphoreType.DMA((size,))] * 2
    return pl.pallas_call(
        functools.partial(reduce_kernel, size, count, extra),
        out_shape=shapes,
        in_specs=[pl.BlockSpec(memory_space=pltpu.VMEM)] * len(operands),
        out_specs=[pl.BlockSpec(memory_space=pltpu.VMEM)] * len(operands),
        scratch_shapes=scratch,
        compiler_params=pltpu.CompilerParams(
            collective_id=collective, has_side_effects=True, vmem_limit_bytes=60 << 20
        ),
        name="reduce_ctx_%d" % collective,
    )(*operands)


def exchange_kernel(size, split, source, target, send, recv, own):
    me = lax.axis_index("ctx")
    lane, row = me % split, me // split
    number = size // split
    greet([{"ctx": ((row + k) % number) * split + lane} for k in range(1, number)])
    mine = pltpu.make_async_copy(source.at[row], target.at[row], own)
    mine.start()
    copies = []
    for k in range(1, number):
        there = (row + k) % number
        copies.append(push(source.at[there], target.at[row], send.at[k], recv.at[k], ctx=there * split + lane))
        copies[-1].start()
    for k in range(1, number):
        here = (row + number - k) % number
        push(source.at[here], target.at[here], send.at[k], recv.at[k], ctx=here * split + lane).wait_recv()
    for copy in copies:
        copy.wait_send()
    mine.wait()


def exchange_ctx(array, size, split, collective):
    return pl.pallas_call(
        functools.partial(exchange_kernel, size, split),
        out_shape=jax.ShapeDtypeStruct(array.shape, array.dtype),
        in_specs=[pl.BlockSpec(memory_space=pl.ANY)],
        out_specs=pl.BlockSpec(memory_space=pl.ANY),
        scratch_shapes=[
            pltpu.SemaphoreType.DMA((size // split,)),
            pltpu.SemaphoreType.DMA((size // split,)),
            pltpu.SemaphoreType.DMA,
        ],
        compiler_params=pltpu.CompilerParams(collective_id=collective, has_side_effects=True),
        name="exchange_ctx_%d" % collective,
    )(array)


def spread_kernel(size, count, *refs):
    sources, pack = refs[:count], refs[count]
    targets, whole = refs[count + 1 : 2 * count + 1], refs[2 * count + 1]
    send, recv, own, send_a, recv_a, send_b, recv_b, own_pack = refs[2 * count + 2 :]
    me, seq = lax.axis_index("ctx"), lax.axis_index("seq")
    greet(
        [{"ctx": (me + k) % size} for k in range(1, size)]
        + [{"seq": core_mate(seq)}, {"seq": row_mate(seq)}]
    )
    rings, local = [], []
    for i in range(count):
        local.append(pltpu.make_async_copy(sources[i], targets[i].at[me], own.at[i]))
        rings.append(RingGather(size, sources[i], targets[i], send.at[i], recv.at[i]))
    local.append(pltpu.make_async_copy(pack.at[me], whole.at[seq, me], own_pack))
    for copy in local:
        copy.start()

    def outward(k):
        there = (me + k) % size
        return push(pack.at[there], whole.at[seq, me], send_a.at[k], recv_a.at[k], ctx=there)

    def inward(k):
        here = (me + size - k) % size
        return push(pack.at[here], whole.at[seq, here], send_a.at[k], recv_a.at[k], ctx=here)

    def sideways(which, k):
        here = (me + size - k) % size
        slab = whole.at[row_mate(seq) if which == 2 else seq, here]
        mate = row_mate(seq) if which == 1 else core_mate(seq)
        return push(slab, slab, send_b.at[which, k], recv_b.at[which, k], seq=mate)

    def landing(which, k):
        here = (me + size - k) % size
        owner = (core_mate(seq), row_mate(seq), core_mate(row_mate(seq)))[which]
        slab = whole.at[owner, here]
        return push(slab, slab, send_b.at[which, k], recv_b.at[which, k], seq=core_mate(seq))

    for ring in rings:
        ring.start(0)
    for k in range(1, size):
        outward(k).start()
    local[-1].wait()
    sideways(1, 0).start()
    sideways(0, 0).start()
    steps = size // 2
    for k in range(1, size):
        if k < steps:
            for ring in rings:
                ring.start(k)
        inward(k).wait_recv()
        sideways(1, k).start()
        sideways(0, k).start()
        landing(1, k - 1).wait_recv()
        sideways(2, k - 1).start()
    landing(1, size - 1).wait_recv()
    sideways(2, size - 1).start()
    for ring in rings:
        ring.finish()
    for copy in local[:-1]:
        copy.wait()
    for k in range(size):
        landing(0, k).wait_recv()
        landing(2, k).wait_recv()
        for which in range(3):
            sideways(which, k).wait_send()
        if k:
            outward(k).wait_send()


def spread_all(arrays, pack, size, rows, collective):
    count = len(arrays)
    shapes = [jax.ShapeDtypeStruct((size,) + a.shape, a.dtype) for a in arrays]
    shapes.append(jax.ShapeDtypeStruct((rows,) + pack.shape, pack.dtype))
    return pl.pallas_call(
        functools.partial(spread_kernel, size, count),
        out_shape=shapes,
        in_specs=[pl.BlockSpec(memory_space=pl.ANY)] * (count + 1),
        out_specs=[pl.BlockSpec(memory_space=pl.ANY)] * (count + 1),
        scratch_shapes=[
            pltpu.SemaphoreType.DMA((count, 2, size // 2)),
            pltpu.SemaphoreType.DMA((count, 2, size // 2)),
            pltpu.SemaphoreType.DMA((count,)),
            pltpu.SemaphoreType.DMA((size,)),
            pltpu.SemaphoreType.DMA((size,)),
            pltpu.SemaphoreType.DMA((3, size)),
            pltpu.SemaphoreType.DMA((3, size)),
            pltpu.SemaphoreType.DMA,
        ],
        compiler_params=pltpu.CompilerParams(collective_id=collective, has_side_effects=True),
        name="spread_all",
    )(*arrays, pack)


def home_kernel(
    size, grads, out, near, from_core, from_row, to_row, to_home,
    load, send_a, recv_a, send_b, recv_b, send_c, recv_c,
):
    me, seq = lax.axis_index("ctx"), lax.axis_index("seq")
    greet(
        [{"ctx": (me + k) % size} for k in range(1, size)]
        + [{"seq": core_mate(seq)}, {"seq": row_mate(seq)}]
    )

    def row_of(which):
        return row_mate(seq) if which == 0 else seq

    def fetch(which, k):
        there = (me + k) % size
        return pltpu.make_async_copy(grads.at[row_of(which), there], near.at[which, k], load.at[which, k])

    def to_core(which, k):
        there = (me + k) % size
        return push(
            grads.at[core_mate(row_of(which)), there], from_core.at[which, k],
            send_a.at[which, k], recv_a.at[which, k], seq=core_mate(seq),
        )

    def across(k):
        return push(to_row.at[k], from_row.at[k], send_b.at[k], recv_b.at[k], seq=row_mate(seq))

    def homeward(k):
        there = (me + k) % size
        return push(to_home.at[k], out.at[me], send_c.at[k], recv_c.at[k], ctx=there)

    def arriving(k):
        here = (me + size - k) % size
        return push(to_home.at[k], out.at[here], send_c.at[k], recv_c.at[k], ctx=here)

    for which in range(2):
        for k in range(size):
            to_core(which, k).start()
            fetch(which, k).start()

    def first(k, _):
        fetch(0, k).wait()
        to_core(0, k).wait_recv()
        to_row[k] = (near[0, k].astype(WIDE) + from_core[0, k].astype(WIDE)).astype(LOW)
        across(k).start()
        return 0

    lax.fori_loop(0, size, first, 0)

    def total(k):
        fetch(1, k).wait()
        to_core(1, k).wait_recv()
        across(k).wait_recv()
        return (near[1, k].astype(WIDE) + from_core[1, k].astype(WIDE) + from_row[k].astype(WIDE)).astype(LOW)

    def second(k, _):
        to_home[k] = total(k)
        homeward(k).start()
        return 0

    lax.fori_loop(1, size, second, 0)
    out[me] = total(0)

    def close(k, _):
        arriving(k).wait_recv()
        homeward(k).wait_send()
        return 0

    lax.fori_loop(1, size, close, 0)

    def drain(k, _):
        to_core(0, k).wait_send()
        to_core(1, k).wait_send()
        across(k).wait_send()
        return 0

    lax.fori_loop(0, size, drain, 0)


def bring_home(grads, size, collective):
    rows, _, height, width = grads.shape
    slab = (size, height, width)
    return pl.pallas_call(
        functools.partial(home_kernel, size),
        out_shape=jax.ShapeDtypeStruct(slab, LOW),
        in_specs=[pl.BlockSpec(memory_space=pl.ANY)],
        out_specs=pl.BlockSpec(memory_space=pltpu.VMEM),
        scratch_shapes=[
            pltpu.VMEM((2,) + slab, LOW),
            pltpu.VMEM((2,) + slab, LOW),
            pltpu.VMEM(slab, LOW),
            pltpu.VMEM(slab, LOW),
            pltpu.VMEM(slab, LOW),
            pltpu.SemaphoreType.DMA((2, size)),
            pltpu.SemaphoreType.DMA((2, size)),
            pltpu.SemaphoreType.DMA((2, size)),
            pltpu.SemaphoreType.DMA((size,)),
            pltpu.SemaphoreType.DMA((size,)),
            pltpu.SemaphoreType.DMA((size,)),
            pltpu.SemaphoreType.DMA((size,)),
        ],
        compiler_params=pltpu.CompilerParams(
            collective_id=collective, has_side_effects=True, vmem_limit_bytes=60 << 20
        ),
        name="bring_home",
    )(grads)


def as_rows(array, lead, width):
    flat = array.reshape(array.shape[:lead] + (-1,))
    short = -flat.shape[-1] % width
    if short:
        flat = jnp.pad(flat, [(0, 0)] * lead + [(0, short)])
    return flat.reshape(flat.shape[:lead] + (-1, width))


def pack_rows(arrays, lead, width):
    pieces = [as_rows(a, lead, width) for a in arrays]
    short = -sum(p.shape[lead] for p in pieces) % 16
    if short:
        pieces.append(jnp.zeros(pieces[0].shape[:lead] + (short, width), pieces[0].dtype))
    return jnp.concatenate(pieces, axis=lead)


def unpack_rows(packed, lead, shapes):
    width, start, parts = packed.shape[-1], 0, []
    for shape in shapes:
        amount = math.prod(shape)
        rows = -(-amount // width)
        piece = lax.slice_in_dim(packed, start, start + rows, axis=lead)
        if rows * width != amount:
            piece = piece.reshape(piece.shape[:lead] + (-1,))[..., :amount]
        parts.append(piece.reshape(packed.shape[:lead] + shape))
        start += rows
    return parts


def rms_scale(values):
    return lax.rsqrt(jnp.mean(values * values, axis=-1, keepdims=True) + NORM_EPS)


def rotate_pairs(values, cosine, sine):
    first, second = jnp.split(values, 2, axis=-1)
    return jnp.concatenate([first * cosine - second * sine, second * cosine + first * sine], axis=-1)


def unrotate_pairs(values, cosine, sine):
    first, second = jnp.split(values, 2, axis=-1)
    return jnp.concatenate([first * cosine + second * sine, second * cosine - first * sine], axis=-1)


def rope_tables(places, factor):
    freqs = 1.0 / ROPE_BASE ** (jnp.arange(0, HEAD_DIM, 2).astype(WIDE) / HEAD_DIM)
    angles = (places.astype(WIDE) / factor)[:, None] * freqs[None, :]
    return jnp.cos(angles), jnp.sin(angles)


def dot(equation, left, right):
    return jnp.einsum(equation, left, right, preferred_element_type=WIDE)


def on_device(
    layer_input, document_ids, expert_routes, rope_factor, attention_gain, feedforward_gain,
    query_weight, key_weight, value_weight, output_weight, router_weight, gate_up, down_weight, cotangent,
):
    nseq, nctx = lax.axis_size("seq"), lax.axis_size("ctx")
    tokens, width = layer_input.shape[1:]
    length = tokens * nctx
    rows, experts, ff2 = gate_up.shape
    ff = ff2 // 2
    down_rows = down_weight.shape[0]
    per_unit = max(1, experts // nctx)
    ff_split = max(1, nctx // experts)
    ff_part = ff // ff_split
    head_split = nctx // KV_HEADS
    unit = lax.axis_index("ctx")
    scale = HEAD_DIM**-0.5

    gu_pack = (
        gate_up.astype(LOW).reshape(rows, experts, 2, ff_split, ff_part).transpose(1, 3, 0, 2, 4)
        .reshape(nctx, per_unit, rows, 2 * ff_part)
    )
    down_pack = jnp.repeat(
        down_weight.astype(LOW).transpose(1, 0, 2), ff_split, axis=0
    ).reshape(nctx, per_unit, down_rows, width)
    out_pack = jnp.broadcast_to(output_weight.astype(LOW)[None], (nctx, rows, width))
    head_pack = jnp.concatenate(
        [
            query_weight.reshape(rows, KV_HEADS, GROUP * HEAD_DIM),
            key_weight.reshape(rows, KV_HEADS, HEAD_DIM),
            value_weight.reshape(rows, KV_HEADS, HEAD_DIM),
        ],
        axis=-1,
    ).astype(LOW).transpose(1, 0, 2)
    head_pack = jnp.repeat(head_pack, head_split, axis=0)
    small_pack = jnp.concatenate(
        [router_weight, attention_gain[:, None], feedforward_gain[:, None]], axis=1
    ).astype(LOW).T.reshape(-1)
    small_pack = jnp.broadcast_to(small_pack[None], (nctx, small_pack.shape[0]))
    shapes = [
        (per_unit, rows, 2 * ff_part), (per_unit, down_rows, width), (rows, width),
        (rows, HEAD_COLS), (experts + 2, rows),
    ]
    pack = pack_rows([gu_pack, down_pack, out_pack, head_pack, small_pack], 1, width)
    documents = jnp.broadcast_to(document_ids.reshape(1, tokens), (16, tokens))

    inputs_all, upstream_all, documents_all, whole = spread_all(
        [layer_input[0], cotangent[0], documents], pack, nctx, nseq, 1
    )
    gu_full, down_full, out_full, head_full, small_full = unpack_rows(whole, 2, shapes)
    gu_full = gu_full.reshape(nseq * nctx, per_unit, rows, 2 * ff_part).transpose(1, 0, 2, 3)
    gu_full = gu_full.reshape(per_unit, width, 2 * ff_part)
    down_full = down_full.reshape(nseq * nctx, per_unit, down_rows, width).transpose(1, 0, 2, 3)
    down_full = down_full.reshape(per_unit, ff, width)
    if ff_split > 1:
        down_full = lax.dynamic_slice_in_dim(down_full, (unit % ff_split) * ff_part, ff_part, 1)
    out_full = out_full.reshape(HEADS * HEAD_DIM, width)
    head_full = head_full.reshape(width, HEAD_COLS)
    small_full = small_full.reshape(nseq * nctx, experts + 2, rows).transpose(1, 0, 2).reshape(experts + 2, width)
    router_full = small_full[:experts]
    gain_one = small_full[experts].astype(WIDE)
    gain_two = small_full[experts + 1].astype(WIDE)

    hidden_all = inputs_all.reshape(length, width).astype(WIDE)
    scale_all = rms_scale(hidden_all)
    normed_all = hidden_all * scale_all
    attend_input = (normed_all * gain_one).astype(LOW)
    heads_pre = dot("td,dj->tj", attend_input, head_full)
    places = jnp.arange(length, dtype=jnp.int32)
    cosine, sine = rope_tables(places, rope_factor[0])
    query_pre = heads_pre[:, : GROUP * HEAD_DIM].reshape(length, GROUP, HEAD_DIM)
    keys = rotate_pairs(heads_pre[:, GROUP * HEAD_DIM : -HEAD_DIM], cosine, sine).astype(LOW)
    values = heads_pre[:, -HEAD_DIM:].astype(LOW)
    queries = rotate_pairs(query_pre, cosine[:, None], sine[:, None]).astype(LOW)
    docs = documents_all[:, 0].reshape(length)

    def my_rows(array):
        if head_split == 1:
            return array
        blocks = array.reshape((nctx // head_split, head_split, tokens) + array.shape[1:])
        picked = lax.dynamic_index_in_dim(blocks, unit % head_split, 1, keepdims=False)
        return picked.reshape((length // head_split,) + array.shape[1:])

    def all_rows(array):
        if head_split == 1:
            return array
        blocks = array.reshape((nctx // head_split, 1, tokens) + array.shape[1:])
        empty = jnp.zeros((nctx // head_split, head_split, tokens) + array.shape[1:], array.dtype)
        start = (0, unit % head_split) + (0,) * (blocks.ndim - 2)
        return lax.dynamic_update_slice(empty, blocks, start).reshape((length,) + array.shape[1:])

    my_queries = my_rows(queries).transpose(1, 0, 2)
    my_docs, my_places = my_rows(docs), my_rows(places)
    allowed = (places[None, :] <= my_places[:, None]) & (docs[None, :] == my_docs[:, None])
    scores = jnp.where(allowed[None], dot("gqd,nd->gqn", my_queries, keys) * scale, NEG_BIG)
    peak = jnp.max(scores, axis=-1, keepdims=True)
    expo = jnp.exp(scores - peak)
    probs = expo / jnp.sum(expo, axis=-1, keepdims=True)
    probs_low = probs.astype(LOW)
    attended = dot("gqn,nd->gqd", probs_low, values)
    head_out = attended.transpose(1, 0, 2).reshape(KV_HEADS, tokens, GROUP * HEAD_DIM).astype(LOW)
    mixed = exchange_ctx(head_out, nctx, head_split, 2)
    mixed_low = mixed.transpose(1, 0, 2).reshape(tokens, HEADS * HEAD_DIM)

    inputs = layer_input[0].astype(WIDE)
    middle = inputs + dot("tj,jd->td", mixed_low, out_full)
    scale_two = rms_scale(middle)
    normed_two = middle * scale_two
    expert_input = (normed_two * gain_two).astype(LOW)
    logits = dot("td,ed->te", expert_input, router_full)
    chosen = jnp.any(
        expert_routes[0][:, :, None] == jnp.arange(experts, dtype=jnp.int32)[None, None, :], axis=1
    )
    picked = jnp.where(chosen, logits, NEG_BIG)
    expo_gate = jnp.where(chosen, jnp.exp(picked - jnp.max(picked, axis=-1, keepdims=True)), 0.0)
    combine = expo_gate / jnp.sum(expo_gate, axis=-1, keepdims=True)

    expert_all, combine_all = gather_ctx([expert_input, combine.T], nctx, 3)
    expert_all = expert_all.reshape(length, width)
    upstream_low = upstream_all.reshape(length, width)
    upstream_wide = upstream_low.astype(WIDE)
    first_expert = unit // ff_split * per_unit
    out_part = jnp.zeros((length, width), WIDE)
    back_part = jnp.zeros((length, width), WIDE)
    gate_grads, gu_grads, down_grads = [], [], []
    for i in range(per_unit):
        weight = lax.dynamic_index_in_dim(combine_all, first_expert + i, 1, keepdims=False).reshape(length, 1)
        gate_and_up = dot("td,df->tf", expert_all, gu_full[i])
        gate, up = gate_and_up[:, :ff_part], gate_and_up[:, ff_part:]
        sigmoid = 1.0 / (1.0 + jnp.exp(-gate))
        activated = gate / (1.0 + jnp.exp(-gate))
        hidden = (activated * up).astype(LOW)
        produced = dot("tf,fd->td", hidden, down_full[i])
        out_part = out_part + weight * produced
        gate_grads.append(jnp.sum(upstream_wide * produced, axis=-1))
        grad_low = (weight * upstream_wide).astype(LOW)
        hidden_grad = dot("td,fd->tf", grad_low, down_full[i])
        down_grads.append(dot("tf,td->fd", hidden, grad_low))
        both = jnp.concatenate(
            [hidden_grad * up * sigmoid * (1.0 + gate * (1.0 - sigmoid)), hidden_grad * activated], axis=-1
        ).astype(LOW)
        gu_grads.append(dot("td,tf->df", expert_all, both))
        back_part = back_part + dot("tf,df->td", both, gu_full[i])
    gate_grad_rows = jnp.stack(gate_grads, axis=0).reshape(per_unit, nctx, tokens).transpose(1, 0, 2)
    gate_grad_rows = jnp.pad(gate_grad_rows, ((0, 0), (0, -per_unit % 8), (0, 0)))
    mix, back_sum, gate_grad_all = reduce_ctx(
        [out_part.astype(LOW).reshape(nctx, tokens, width), back_part.astype(LOW).reshape(nctx, tokens, width)],
        nctx, 4, small=gate_grad_rows,
    )

    layer_output = (middle + mix).astype(LOW)[None]
    upstream = cotangent[0].astype(WIDE)
    gate_grad = gate_grad_all[:, :per_unit].reshape(experts, ff_split, tokens).sum(axis=1).T
    gate_grad = jnp.where(chosen, gate_grad, 0.0)
    select_grad = combine * (gate_grad - jnp.sum(combine * gate_grad, axis=-1, keepdims=True))
    logit_grad = select_grad.astype(LOW)
    back_two = back_sum + dot("te,ed->td", logit_grad, router_full)
    router_part = dot("te,td->ed", logit_grad, expert_input)
    gain_two_part = jnp.sum(back_two * normed_two, axis=0)
    normed_two_grad = back_two * gain_two
    middle_grad = upstream + scale_two * (
        normed_two_grad - normed_two * jnp.mean(normed_two_grad * normed_two, axis=-1, keepdims=True)
    )
    project_grad = middle_grad.astype(LOW)
    out_grad_part = dot("tj,td->jd", mixed_low, project_grad)
    mixed_grad = dot("td,jd->tj", project_grad, out_full).astype(LOW)
    mixed_grad = mixed_grad.reshape(tokens, KV_HEADS, GROUP * HEAD_DIM).transpose(1, 0, 2)

    head_grad = exchange_ctx(mixed_grad, nctx, head_split, 5)
    head_grad = head_grad.reshape(length // head_split, GROUP, HEAD_DIM).transpose(1, 0, 2)
    delta = jnp.sum(head_grad.astype(WIDE) * attended, axis=-1, keepdims=True)
    value_grad = dot("gqn,gqd->nd", probs_low, head_grad)
    prob_grad = dot("gqd,nd->gqn", head_grad, values)
    score_grad = (probs * (prob_grad - delta)).astype(LOW)
    query_grad = dot("gqn,nd->gqd", score_grad, keys) * scale
    key_grad = dot("gqn,gqd->nd", score_grad, my_queries) * scale
    cos_q, sin_q = my_rows(cosine)[:, None], my_rows(sine)[:, None]
    query_pre_grad = unrotate_pairs(query_grad.transpose(1, 0, 2), cos_q, sin_q)
    query_pre_grad = all_rows(query_pre_grad.reshape(length // head_split, GROUP * HEAD_DIM))
    key_pre_grad = unrotate_pairs(key_grad, cosine, sine)
    heads_grad = jnp.concatenate([query_pre_grad, key_pre_grad, value_grad], axis=-1).astype(LOW)
    head_grads = dot("td,tj->dj", attend_input, heads_grad)
    attend_grad = dot("tj,dj->td", heads_grad, head_full)
    gain_one_part = jnp.sum(attend_grad * normed_all, axis=0)

    small_grads = jnp.concatenate([router_part, gain_one_part[None], gain_two_part[None]], axis=0)
    down_stack = jnp.stack(down_grads)
    if ff_split > 1:
        down_stack = lax.dynamic_update_slice_in_dim(
            jnp.zeros((per_unit, ff, width), WIDE), down_stack, (unit % ff_split) * ff_part, 1
        )
    grads = pack_rows(
        [
            jnp.stack(gu_grads).astype(LOW).reshape(per_unit, nseq, nctx, rows, 2 * ff_part).transpose(1, 2, 0, 3, 4),
            down_stack.astype(LOW).reshape(per_unit, nseq, nctx, down_rows, width).transpose(1, 2, 0, 3, 4),
            out_grad_part.astype(LOW).reshape(nseq, nctx, rows, width),
            head_grads.astype(LOW).reshape(nseq, nctx, rows, HEAD_COLS),
            small_grads.astype(LOW).reshape(experts + 2, nseq, nctx, rows).transpose(1, 2, 0, 3),
        ],
        2,
        width,
    )
    (attend_sum,) = reduce_ctx([attend_grad.astype(LOW).reshape(nctx, tokens, width)], nctx, 6)
    landed = bring_home(grads, nctx, 7)
    gu_home, down_home, out_home, head_home, small_home = [p.astype(WIDE) for p in unpack_rows(landed, 1, shapes)]
    gate_up_gradient = (
        gu_home.reshape(experts, ff_split, rows, 2, ff_part).transpose(2, 0, 3, 1, 4).reshape(rows, experts, ff2)
    )
    down_gradient = down_home.reshape(experts, ff_split, down_rows, width).sum(axis=1).transpose(1, 0, 2)
    output_gradient = out_home.sum(axis=0)
    head_home = head_home.reshape(KV_HEADS, head_split, rows, HEAD_COLS).sum(axis=1).transpose(1, 0, 2)
    query_gradient = head_home[..., : GROUP * HEAD_DIM].reshape(rows, HEADS * HEAD_DIM)
    key_gradient = head_home[..., GROUP * HEAD_DIM : -HEAD_DIM].reshape(rows, KV_HEADS * HEAD_DIM)
    value_gradient = head_home[..., -HEAD_DIM:].reshape(rows, KV_HEADS * HEAD_DIM)
    small_home = small_home.sum(axis=0)
    router_gradient = small_home[:experts].T

    scale_one = rms_scale(inputs)
    normed_one = inputs * scale_one
    normed_one_grad = attend_sum * gain_one
    input_gradient = (
        middle_grad
        + scale_one
        * (normed_one_grad - normed_one * jnp.mean(normed_one_grad * normed_one, axis=-1, keepdims=True))
    ).astype(LOW)[None]
    return (
        layer_output, input_gradient, small_home[experts], small_home[experts + 1],
        query_gradient, key_gradient, value_gradient, output_gradient, router_gradient,
        gate_up_gradient, down_gradient,
    )


def solution(mesh):
    both = ("seq", "ctx")
    return jax.shard_map(
        on_device,
        mesh=mesh,
        in_specs=(
            P("seq", "ctx", None), P("seq", "ctx"), P("seq", "ctx", None), P(), P(both), P(both),
            P(both, None), P(both, None), P(both, None), P(both, None), P(both, None),
            P(both, None, None), P(both, None, None), P("seq", "ctx", None),
        ),
        out_specs=(
            P("seq", "ctx", None), P("seq", "ctx", None), P(both), P(both),
            P(both, None), P(both, None), P(both, None), P(both, None), P(both, None),
            P(both, None, None), P(both, None, None),
        ),
        check_vma=False,
    )
```

time: 3700 us -> 542 us (0.15)
  waiting for transfers between devices: 3170 us -> 0 us
  Pallas kernels: 0 us -> 324 us
  blocking collectives: 166 us -> 0 us
  local copies, waits for them, and re-layouts: 170 us -> 105 us
  matrix products: 135 us -> 72.5 us
    reduce_scatter x6 -> x0, waiting for transfers between devices: 2610 us -> none  [the longest x1 1410 us: on_device(): lax.psum_scatter(jnp.einsum('ecr,ecf->ref', columns, both_grad, preferred...]
    all_gather x8 -> x0, waiting for transfers between devices: 425 us -> none  [the longest x1 180 us: on_device(): lax.all_gather(gate_up_low, ('seq', 'ctx'), axis=0, tiled=True)]
    pallas_call x0 -> x7, Pallas kernels: none -> 324 us  [the longest x1 121 us: spread_all(): pl.pallas_call(functools.partial(spread_kernel, size, count), out_shape=s...]
    unnamed x20 -> x0, waiting for transfers between devices: 133 us -> none
    transpose x2 -> x6, local copies, waits for them, and re-layouts: 98.9 us -> 6.79 us  [the longest x1 2.53 us: on_device(): jnp.stack(gu_grads).astype(LOW)]
    all_gather x2 -> x0, blocking collectives: 83.7 us -> none  [the longest x1 67.4 us: on_device(): lax.all_gather(router_weight.astype(jnp.bfloat16), ('seq', 'ctx'), axis=0...]
    unnamed x2 -> x0, blocking collectives: 82.2 us -> none
    dot_general x27 -> x26, matrix products: 134 us -> 67.1 us  [dot(): return jnp.einsum(equation, left, right, preferred_element_type=WIDE)]
  transfers between devices with their start and end apart: 17 -> 0, of which waited for: 14 -> 0; matrix products, arithmetic and copies ran while one was open for 6% -> 0% of each run, Pallas kernels for 0% -> 0%
where the time goes in v1:
time: 542 us; the launch traced here: 533 us
  Pallas kernels  324 us (60%)
  local copies, waits for them, and re-layouts  105 us (19%)
  matrix products  72.5 us (13%)
  other arithmetic  28.6 us (5%)
    pallas_call x1, Pallas kernels, spread_all(): pl.pallas_call(functools.partial(spread_kernel, size, count), out_shape=s...  121 us
    pallas_call x2, Pallas kernels, reduce_ctx(): pl.pallas_call(functools.partial(reduce_kernel, size, count, extra), out_...  78.7 us
    pallas_call x1, Pallas kernels, bring_home(): pl.pallas_call(functools.partial(home_kernel, size), out_shape=jax.ShapeD...  74.4 us
    dot_general x26, matrix products, dot(): return jnp.einsum(equation, left, right, preferred_element_type=WIDE)  67.1 us
    concatenate x2, local copies, waits for them, and re-layouts, pack_rows(): return jnp.concatenate(pieces, axis=lead)  44.6 us
    pallas_call x1, Pallas kernels, gather_ctx(): pl.pallas_call(functools.partial(gather_kernel, size, count), out_shape=[...  27.6 us
    pallas_call x2, Pallas kernels, exchange_ctx(): pl.pallas_call(functools.partial(exchange_kernel, size, split), out_shape...  22.1 us

profile of v1, /device:TPU:0, one launch (start us, length us, event | category | flops | bytes accessed | tf_op | source)
XLA Modules:
  0.0 533.4 jit_solution(11564570963359546096)
XLA Ops:
  2.2 1.8 convert_element_type.199
  4.7 1.0 copy.134
  8.4 7.0 %concatenate.56.refs_3_ = bf16[8,144,1024]{2,1,0:T(8,128)(2,1)} concatenate(bf16[8,64,1024]{2,1,0:T(8,128)(2,1)S(1)} %reshape_reshape_reshape.9, bf16[8,32,1024]{2,1,0:T(8,128)(2,1)S(1)} %bitcast.279, bf16[8,32,1024]{2,1,0:T(8,128)(2,1)S(1)} %broadcast_in_dim.48, bf16[8,8,1024]{2,1,0:T(8,128)(2,1)S(1)} %reshape_reshape_reshape_broadcast_in_dim.3, ...), dimensions={1} | concatenate | bytes 4718592 | tf_op jit(solution)/shard_map/concatenate | solution.py:501
  15.9 121.3 %spread_all.1 = (bf16[8,128,1024]{2,1,0:T(8,128)(2,1)}, bf16[8,128,1024]{2,1,0:T(8,128)(2,1)}, s32[8,16,128]{2,1,0:T(8,128)}, bf16[4,8,144,1024]{3,2,1,0:T(8,128)(2,1)}) custom-call(bf16[128,1024]{1,0:T(8,128)(2,1)} %bitcast.271, bf16[128,1024]{1,0:T(8,128)(2,1)} %bitcast.306, s32[16,128]{1,0:T(8,128)} %broadcast_in_dim.47.refs_2_, ...), custom_call_target="tpu_custom_call" | custom-call | tf_op jit(solution)/shard_map/spread_all/pallas_call | solution.py:360
  137.3 1.1 slice.128
  139.3 2.2 multiply_reduce_fusion.1
  142.7 1.1 slice.131
  143.8 1.1 reshape_reshape.19
  144.9 1.8 fusion.97
  149.6 5.4 %fusion.95 = (f32[2,1024]{1,0:T(2,128)S(1)}, f32[2,1024,1024]{1,2,0:T(8,128)}) fusion(pred[1024,1024]{0,1:T(8,128)(4,1)S(1)} %fusion.8, bf16[1024,2,32]{0,2,1:T(8,128)(2,1)S(1)} %get-tuple-element.58, bf16[1024,2,32]{0,2,1:T(8,128)(2,1)S(1)} %get-tuple-element.57, bf16[1024,32]{0,1:T(8,128)(2,1)S(1)} %get-tuple-element.54, ...), kind=kOutput, calls=%fused_computation.185 | convolution fusion | flops 277611520 | bytes 9838592 | tf_op jit(solution)/shard_map/sub | solution.py:636
  155.0 4.6 fusion.10
  159.7 2.2 fusion.96
  162.0 0.9 copy.86.source
  162.9 14.9 %exchange_ctx_2.1 = bf16[8,128,128]{2,1,0:T(8,128)(2,1)} custom-call(bf16[8,128,128]{2,1,0:T(8,128)(2,1)} %copy.86.source), custom_call_target="tpu_custom_call" | custom-call | tf_op jit(solution)/shard_map/exchange_ctx_2/pallas_call | solution.py:272
  177.8 1.1 copy.87
  179.0 4.5 fusion.90
  185.5 27.6 %gather_ctx_3.1 = (bf16[8,128,1024]{2,1,0:T(8,128)(2,1)}, f32[8,16,128]{2,1,0:T(8,128)}) custom-call(bf16[128,1024]{1,0:T(8,128)(2,1)} %copy-done.9, f32[16,128]{1,0:T(8,128)} %fusion.71.refs_1_), custom_call_target="tpu_custom_call" | custom-call | tf_op jit(solution)/shard_map/gather_ctx_3/pallas_call | solution.py:123
  213.1 2.6 slice.138
  215.8 1.9 fusion.91
  217.7 4.4 fusion.98
  223.0 2.4 fusion.3
  225.6 1.2 copy-done.21
  226.8 2.3 copy-done.61
  229.1 2.0 multiply_convert_fusion.6
  231.3 14.1 %fusion.99 = f32[1024,1024]{0,1:T(8,128)S(1)} fusion(bf16[1024,1024]{1,0:T(8,128)(2,1)S(1)} %bitcast.282, bf16[1024,1024]{1,0:T(8,128)(2,1)S(1)} %bitcast.292), kind=kOutput, calls=%fused_computation.189 | convolution fusion | flops 2147483648 | bytes 8388608 | tf_op jit(solution)/shard_map/td,df->tf/dot_general | solution.py:538
  245.4 2.0 multiply_convert_fusion.4
  247.4 1.3 fusion.100
  248.8 1.4 copy-done.23
  250.2 3.2 fusion.4
  254.0 2.4 fusion.23
  256.4 3.7 add_convert_fusion
  260.2 44.4 %reduce_ctx_4.1 = (f32[128,1024]{1,0:T(8,128)}, f32[128,1024]{1,0:T(8,128)}, f32[8,8,128]{2,1,0:T(8,128)}) custom-call(bf16[8,128,1024]{2,1,0:T(8,128)(2,1)} %bitcast.287, bf16[8,128,1024]{2,1,0:T(8,128)(2,1)} %bitcast.288, f32[8,8,128]{2,1,0:T(8,128)} %pad.13.refs_2_), custom_call_target="tpu_custom_call" | custom-call | tf_op jit(solution)/shard_map/reduce_ctx_4/pallas_call | solution.py:238
  306.4 1.4 multiply_reduce_fusion.2
  307.9 1.9 multiply_add_fusion
  309.8 1.5 convolution_convert_fusion.4
  311.3 1.1 copy.89
  313.3 7.2 %exchange_ctx_5.1 = bf16[8,128,128]{2,1,0:T(8,128)(2,1)} custom-call(bf16[8,128,128]{2,1,0:T(8,128)(2,1)} %bitcast.303), custom_call_target="tpu_custom_call" | custom-call | tf_op jit(solution)/shard_map/exchange_ctx_5/pallas_call | solution.py:272
  320.5 1.1 copy.91
  322.5 4.8 multiply_convert_fusion
  328.4 1.4 fusion.25
  330.7 1.6 fusion.26
  332.4 3.4 multiply_reduce_fusion
  336.3 2.4 convolution_convert_fusion.3
  338.8 1.1 reshape_reshape_reshape.11
  340.6 0.9 copy-done.22
  341.5 2.7 fusion.21
  344.2 1.3 fusion.22
  345.6 1.5 copy.100
  347.1 3.9 copy.96
  351.1 4.7 convert_bitcast_fusion.1
  355.8 2.4 convert_bitcast_fusion
  358.6 2.5 copy.99
  362.0 37.6 %concatenate.67.grads = bf16[4,8,144,1024]{3,2,1,0:T(8,128)(2,1)} concatenate(bf16[4,8,64,1024]{3,2,1,0:T(8,128)(2,1)} %bitcast.264, bf16[4,8,32,1024]{3,2,1,0:T(8,128)(2,1)} %bitcast.267, bf16[4,8,32,1024]{3,2,1,0:T(8,128)(2,1)S(1)} %bitcast.266, bf16[4,8,8,1024]{3,2,1,0:T(8,128)(2,1)S(1)} %copy-done.16, bf16[4,8,1,1024]{3,2,1,0:T(2,128)(2,1)S(1)} %copy.104, ...), dimensions={2} | concatenate | bytes 18874368 | tf_op jit(solution)/shard_map/concatenate | solution.py:501
  399.6 74.4 %bring_home.1 = bf16[8,144,1024]{2,1,0:T(8,128)(2,1)} custom-call(bf16[4,8,144,1024]{3,2,1,0:T(8,128)(2,1)} %concatenate.67.grads), custom_call_target="tpu_custom_call" | custom-call | tf_op jit(solution)/shard_map/bring_home/pallas_call | solution.py:462
  474.0 2.8 slice_convert_fusion
  476.8 3.0 reshape.464
  479.8 2.8 reshape.473
  482.6 4.2 copy.121
  486.8 1.3 copy.133
  491.3 1.8 convert_reduce_fusion
  493.1 0.9 slice.149
  495.3 34.3 %reduce_ctx_6.1 = f32[128,1024]{1,0:T(8,128)} custom-call(bf16[8,128,1024]{2,1,0:T(8,128)(2,1)} %bitcast.278), custom_call_target="tpu_custom_call" | custom-call | tf_op jit(solution)/shard_map/reduce_ctx_6/pallas_call | solution.py:238
  529.7 1.3 fusion.31
  531.0 2.0 fusion.38
  (227 shorter events, 26.3 us)
Async XLA Ops:
  4.7 1.8 copy-start.32
  5.7 1.2 copy-start.50
  6.5 1.5 copy-start.46
  6.5 1.7 copy-start.47
  8.3 7.0 %copy-start.59 = (s32[1,128]{1,0:T(1,128)S(1)}, s32[1,128]{1,0:T(1,128)}, u32[]{:S(2)}) copy-start(s32[1,128]{1,0:T(1,128)} %param.15) | copy-start | bytes 1540
  138.6 3.6 copy-start.33
  139.3 2.8 copy-start.3
  146.7 13.0 %copy-start.8 = (f32[1024,256]{0,1:T(8,128)}, f32[1024,256]{0,1:T(8,128)S(1)}, u32[]{:S(2)}) copy-start(f32[1024,256]{0,1:T(8,128)S(1)} %fusion.97) | copy-start | bytes 3145732
  148.0 7.0 %copy-start.30 = (f32[1024,32]{0,1:T(8,128)}, f32[1024,32]{0,1:T(8,128)S(1)}, u32[]{:S(2)}) copy-start(f32[1024,32]{0,1:T(8,128)S(1)} %get-tuple-element.68) | copy-start | bytes 393220
  148.0 7.0 %copy-start.41 = (bf16[1024,32]{0,1:T(8,128)(2,1)}, bf16[1024,32]{0,1:T(8,128)(2,1)S(1)}, u32[]{:S(2)}) copy-start(bf16[1024,32]{0,1:T(8,128)(2,1)S(1)} %get-tuple-element.53) | copy-start | bytes 196612
  148.0 7.0 %copy-start.43 = (bf16[1024,32]{0,1:T(8,128)(2,1)}, bf16[1024,32]{0,1:T(8,128)(2,1)S(1)}, u32[]{:S(2)}) copy-start(bf16[1024,32]{0,1:T(8,128)(2,1)S(1)} %get-tuple-element.54) | copy-start | bytes 196612
  148.2 6.9 %copy-start.37 = (bf16[1024,2,32]{0,2,1:T(8,128)(2,1)}, bf16[1024,2,32]{0,2,1:T(8,128)(2,1)S(1)}, u32[]{:S(2)}) copy-start(bf16[1024,2,32]{0,2,1:T(8,128)(2,1)S(1)} %get-tuple-element.57) | copy-start | bytes 393220
  148.2 6.9 %copy-start.39 = (bf16[1024,2,32]{0,2,1:T(8,128)(2,1)}, bf16[1024,2,32]{0,2,1:T(8,128)(2,1)S(1)}, u32[]{:S(2)}) copy-start(bf16[1024,2,32]{0,2,1:T(8,128)(2,1)S(1)} %get-tuple-element.58) | copy-start | bytes 393220
  155.0 4.7 copy-start.52
  159.7 2.2 copy-start
  179.0 4.5 copy-start.13
  179.0 4.5 copy-start.6
  183.5 1.2 copy-start.56
  184.0 122.4 %copy-start.54 = (f32[128]{0:T(128)}, f32[128]{0:T(128)S(1)}, u32[]{:S(2)}) copy-start(f32[128]{0:T(128)S(1)} %add_rsqrt_fusion.2) | copy-start | bytes 1540
  184.4 1.1 copy-start.9
  215.8 1.9 copy-start.17
  217.7 4.5 copy-start.26
  223.0 2.4 copy-start.5
  225.4 1.4 copy-start.21
  225.4 20.0 %copy-start.19 = (bf16[8,128,1024]{2,1,0:T(8,128)(2,1)}, bf16[8,128,1024]{2,1,0:T(8,128)(2,1)S(1)}, u32[]{:S(2)}) copy-start(bf16[8,128,1024]{2,1,0:T(8,128)(2,1)S(1)} %get-tuple-element.49) | copy-start | bytes 6291460
  225.4 3.7 copy-start.61
  229.1 2.0 copy-start.18
  229.1 2.2 copy-start.25
  231.1 17.7 %copy-start.60 = (bf16[1024,512]{0,1:T(8,128)(2,1)}, bf16[1024,512]{0,1:T(8,128)(2,1)S(1)}, u32[]{:S(2)}) copy-start(bf16[1024,512]{0,1:T(8,128)(2,1)S(1)} %get-tuple-element.45) | copy-start | bytes 3145732
  231.1 22.9 %copy-start.62 = (bf16[1024,512]{0,1:T(8,128)(2,1)}, bf16[1024,512]{0,1:T(8,128)(2,1)S(1)}, u32[]{:S(2)}) copy-start(bf16[1024,512]{0,1:T(8,128)(2,1)S(1)} %get-tuple-element.40) | copy-start | bytes 3145732
  231.1 22.9 %copy-start.63 = (bf16[1024,512]{0,1:T(8,128)(2,1)}, bf16[1024,512]{0,1:T(8,128)(2,1)S(1)}, u32[]{:S(2)}) copy-start(bf16[1024,512]{0,1:T(8,128)(2,1)S(1)} %get-tuple-element.41) | copy-start | bytes 3145732
  247.4 1.3 copy-start.28
  247.4 9.0 %copy-start.64 = (bf16[1024,512]{0,1:T(8,128)(2,1)}, bf16[1024,512]{0,1:T(8,128)(2,1)S(1)}, u32[]{:S(2)}) copy-start(bf16[1024,512]{0,1:T(8,128)(2,1)S(1)} %get-tuple-element.38) | copy-start | bytes 3145732
  247.4 9.0 %copy-start.66 = (bf16[1024,512]{0,1:T(8,128)(2,1)}, bf16[1024,512]{0,1:T(8,128)(2,1)S(1)}, u32[]{:S(2)}) copy-start(bf16[1024,512]{0,1:T(8,128)(2,1)S(1)} %get-tuple-element.39) | copy-start | bytes 3145732
  247.4 2.7 copy-start.23
  250.2 3.9 copy-start.27
  260.2 45.2 %copy-start.10 = (bf16[128,1024]{1,0:T(8,128)(2,1)S(1)}, bf16[128,1024]{1,0:T(8,128)(2,1)}, u32[]{:S(2)}) copy-start(bf16[128,1024]{1,0:T(8,128)(2,1)} %copy-done.9) | copy-start | bytes 786436
  305.7 2.2 copy-start.35
  309.8 12.0 %copy-start.7 = (f32[2,1024,64]{1,2,0:T(8,128)S(1)}, f32[2,1024,64]{1,2,0:T(8,128)}, u32[]{:S(2)}) copy-start(f32[2,1024,64]{1,2,0:T(8,128)} %get-tuple-element.76) | copy-start | bytes 1572868
  311.3 11.2 %copy-start.53 = (f32[2,1024]{1,0:T(2,128)S(1)}, f32[2,1024]{1,0:T(2,128)}, u32[]{:S(2)}) copy-start(f32[2,1024]{1,0:T(2,128)} %copy-done.52) | copy-start | bytes 24580
  322.5 4.8 copy-start.42
  322.5 4.8 copy-start.44
  327.4 1.0 copy-start.38
  327.4 1.0 copy-start.40
  328.4 3.9 copy-start.45
  328.4 1.4 copy-start.58
  328.4 2.3 copy-start.1
  328.4 2.3 copy-start.12
  330.4 1.9 copy-start.48
  330.4 1.9 copy-start.49
  330.7 1.6 copy-start.4
  330.7 1.7 copy-start.15
  330.7 1.7 copy-start.55
  332.4 3.6 copy-start.36
  336.3 3.6 copy-start.14
  339.9 1.6 copy-start.22
  341.5 2.7 copy-start.20
  341.5 2.7 copy-start.29
  351.1 4.7 copy-start.24
  351.1 4.7 copy-start.65
  351.1 4.7 copy-start.67
  358.6 3.4 copy-start.16
  482.6 4.2 slice-start
  486.8 2.0 copy-start.2
  (5 other events, 4.0 us)
